TPU v7x, 256 devices: a whole 4x4x8 slice. The times are simulated.
256 devices in a mesh: dp: 8 (over y, z_hi), tm: 4 (over x), height: 8 (over z_lo, core).
Axes of the slice: x: 4, y: 4, z: 8 (z_hi: 2, z_lo: 4; z = z_hi * 4 + z_lo), core: 2. Of those that a mesh axis runs over, the one named last changes fastest.
Arguments:
- low_frames: bfloat16 [8, 16, 32, 32, 256], P('dp', 'tm', 'height'), may hold values from -6 to 6
- spatial_weight: bfloat16 [3, 3, 256, 256], replicated, may hold values from -0.125 to 0.125
- temporal_weight: bfloat16 [3, 256, 256], replicated, may hold values from -0.21875 to 0.21875
- cotangent: bfloat16 [8, 16, 64, 64, 256], P('dp', 'tm', 'height'), may hold values from -6 to 6
Outputs:
- section_out: bfloat16 [8, 16, 64, 64, 256], P('dp', 'tm', 'height')
- input_grad: bfloat16 [8, 16, 32, 32, 256], P('dp', 'tm', 'height')
- spatial_grad: float32 [3, 3, 256, 256], replicated
- temporal_grad: float32 [3, 256, 256], replicated
All inputs are finite; a program needn't handle non-finite values.
Results may differ from a plain program's by a relative error of at most 0.0033.
Values may be sent and summed in bfloat16 or wider, within the bound.
A program may use at most 64 MiB of HBM per device.

v0:
```python
import jax
import jax.numpy as jnp
from jax import lax
from jax.sharding import PartitionSpec as P


def extended(block, sides, width):
    for axis, dim in sides:
        count = lax.axis_size(axis)
        forward = [(i, i + 1) for i in range(count - 1)]
        backward = [(target, source) for source, target in forward]
        low = lax.ppermute(
            lax.slice_in_dim(block, block.shape[dim] - width, None, axis=dim), axis, forward
        )
        high = lax.ppermute(lax.slice_in_dim(block, 0, width, axis=dim), axis, backward)
        block = jnp.concatenate([low, block, high], axis=dim)
    return block


def shifted(block, axis, distance):
    devices = range(lax.axis_size(axis))
    route = [(i - distance, i) for i in devices if i - distance in devices]
    return lax.ppermute(block, axis, route)


def spatial_apply(padded, weights, rows, cols):
    chan = weights.shape[-1]
    total = jnp.zeros((padded.shape[0] * rows * cols, chan), jnp.float32)
    for i in range(3):
        for j in range(3):
            piece = padded[:, i : i + rows, j : j + cols, :].reshape(-1, chan)
            total = total + jnp.dot(piece, weights[i, j], preferred_element_type=jnp.float32)
    return total


def on_device(low_frames, spatial_weight, temporal_weight, cotangent):
    low = low_frames[0]
    grad_out = cotangent[0]
    frames, rows_low, cols_low, chan = low.shape
    rows = 2 * rows_low
    cols = 2 * cols_low
    low_ext = extended(low, (("height", 1),), 1)
    upsampled = jnp.repeat(jnp.repeat(low_ext, 2, axis=1), 2, axis=2)[:, 1:-1]
    padded = jnp.pad(upsampled, ((0, 0), (0, 0), (1, 1), (0, 0)))
    pre = spatial_apply(padded, spatial_weight, rows, cols)
    act = jax.nn.silu(pre).astype(jnp.bfloat16).reshape(frames, rows, cols, chan)
    earlier = shifted(act[frames - 2 :], "tm", 1)
    act_ext = jnp.concatenate([earlier, act], 0)
    mixed = padded[:, 1:-1, 1:-1, :].reshape(-1, chan).astype(jnp.float32)
    for k in range(3):
        mixed = mixed + jnp.dot(
            act_ext[2 - k : 2 - k + frames].reshape(-1, chan),
            temporal_weight[k],
            preferred_element_type=jnp.float32,
        )
    section_out = mixed.astype(jnp.bfloat16).reshape(1, frames, rows, cols, chan)
    later = shifted(grad_out[:2], "tm", -1)
    grad_ext = jnp.concatenate([grad_out, later], 0)
    grad_flat = grad_out.reshape(-1, chan)
    act_grad = jnp.zeros((frames * rows * cols, chan), jnp.float32)
    tgrads = []
    for k in range(3):
        act_grad = act_grad + jnp.dot(
            grad_ext[k : k + frames].reshape(-1, chan),
            temporal_weight[k].T,
            preferred_element_type=jnp.float32,
        )
        tgrads.append(
            lax.dot_general(
                act_ext[2 - k : 2 - k + frames].reshape(-1, chan),
                grad_flat,
                (((0,), (0,)), ((), ())),
                preferred_element_type=jnp.float32,
            )
        )
    temporal_grad = jnp.stack(tgrads)
    sig = jax.nn.sigmoid(pre)
    pre_grad = (act_grad * (sig * (1.0 + pre * (1.0 - sig)))).astype(jnp.bfloat16)
    sgrads = []
    for i in range(3):
        for j in range(3):
            piece = padded[:, i : i + rows, j : j + cols, :].reshape(-1, chan)
            sgrads.append(
                lax.dot_general(
                    piece, pre_grad, (((0,), (0,)), ((), ())), preferred_element_type=jnp.float32
                )
            )
    spatial_grad = jnp.stack(sgrads).reshape(3, 3, chan, chan)
    grad_rows = extended(pre_grad.reshape(frames, rows, cols, chan), (("height", 1),), 1)
    grad_pad = jnp.pad(grad_rows, ((0, 0), (0, 0), (1, 1), (0, 0)))
    total = grad_flat.astype(jnp.float32)
    for i in range(3):
        for j in range(3):
            piece = grad_pad[:, 2 - i : 2 - i + rows, 2 - j : 2 - j + cols, :].reshape(-1, chan)
            total = total + jnp.dot(
                piece, spatial_weight[i, j].T, preferred_element_type=jnp.float32
            )
    input_grad = (
        total.reshape(frames, rows_low, 2, cols_low, 2, chan).sum(axis=(2, 4)).astype(jnp.bfloat16)
    )
    spatial_grad, temporal_grad = lax.psum((spatial_grad, temporal_grad), ("dp", "tm", "height"))
    return (section_out, input_grad[None], spatial_grad, temporal_grad)


def solution(mesh):
    in_specs = (P("dp", "tm", "height", None, None), P(), P(), P("dp", "tm", "height", None, None))
    out_specs = (P("dp", "tm", "height", None, None), P("dp", "tm", "height", None, None), P(), P())
    return jax.shard_map(
        on_device, mesh=mesh, in_specs=in_specs, out_specs=out_specs, check_vma=False
    )
```

profile of v0, /device:TPU:1, one launch (start us, length us, event | category | flops | bytes accessed | tf_op | source)
XLA Modules:
  0.0 336.0 jit_solution(3014307268936639082)
XLA Ops:
  7.2 0.9 fusion.77
  8.1 4.9 %collective-permute-start = (bf16[4,1,32,256]{3,2,1,0:T(8,128)(2,1)S(1)}, bf16[4,1,32,256]{3,2,1,0:T(8,128)(2,1)S(1)}, u32[]{:S(2)}, u32[]{:S(2)}) collective-permute-start(bf16[4,1,32,256]{3,2,1,0:T(8,128)(2,1)S(1)} %get-tuple-element.29), channel_id=1, source_target_pairs={{0,1},{1,2},{2,3},{3,4},{4,5},{5,6},{6,7},{8,9},{9,10},{10,11},{11... | collective-permute-start | bytes 196616 | tf_op jit(solution)/shard_map/ppermute | solution.py:12
  13.0 2.1 collective-permute-start.1
  15.1 1.9 slice_bitcast_fusion
  17.0 1.3 collective-permute-start.3
  18.3 3.0 fusion.26
  21.5 1.4 broadcast_in_dim.8
  24.0 4.2 %pad_slice_fusion.4 = (bf16[4,8,64,256]{3,2,1,0:T(8,128)(2,1)S(1)}, bf16[4,8,64,256]{3,2,1,0:T(8,128)(2,1)S(1)}, bf16[4,8,64,256]{3,2,1,0:T(8,128)(2,1)S(1)}, bf...) fusion(bf16[4,10,64,256]{3,2,1,0:T(8,128)(2,1)S(1)} %slice.207), kind=kLoop, calls=%fused_computation.66 | loop fusion | bytes 7602176 | tf_op jit(solution)/shard_map/slice | solution.py:31
  31.7 0.7 multiply_convert_fusion
  32.5 4.1 %collective-permute-start.2 = (bf16[2,8,64,256]{3,2,1,0:T(8,128)(2,1)S(1)}, bf16[2,8,64,256]{3,2,1,0:T(8,128)(2,1)S(1)}, u32[]{:S(2)}, u32[]{:S(2)}) collective-permute-start(bf16[2,8,64,256]{3,2,1,0:T(8,128)(2,1)S(1)} %bitcast.235), channel_id=1, source_target_pairs={{0,8},{8,16},{16,24},{1,9},{9,17},{17,25},{2,10},{10,18},{18,26},{... | collective-permute-start | bytes 1572872 | tf_op jit(solution)/shard_map/ppermute | solution.py:23
  37.6 1.4 pad_maximum_fusion.2
  39.9 1.1 fusion.4
  42.2 4.2 %collective-permute-start.4 = (bf16[4,1,64,256]{3,2,1,0:T(8,128)(2,1)}, bf16[4,1,64,256]{3,2,1,0:T(8,128)(2,1)S(1)}, u32[]{:S(2)}, u32[]{:S(2)}) collective-permute-start(bf16[4,1,64,256]{3,2,1,0:T(8,128)(2,1)} %get-tuple-element.27), channel_id=1, source_target_pairs={{0,1},{1,2},{2,3},{3,4},{4,5},{5,6},{6,7},{8,9},{9,10},{10,11},{11... | collective-permute-start | bytes 393224 | tf_op jit(solution)/shard_map/ppermute | solution.py:12
  46.4 2.1 collective-permute-start.5
  53.1 0.7 copy-done.3
  54.8 1.4 fusion.5
  56.2 0.9 pad_maximum_fusion.4
  57.2 0.8 fusion.10
  58.0 1.1 fusion.75
  63.6 2.5 reshape.142
  66.0 4.0 %reduce_sum.9 = bf16[4,4,32,256]{3,2,1,0:T(8,128)(2,1)} reduce(f32[4,4,2,32,2,256]{5,4,3,2,1,0:T(2,128)} %reshape.142, f32[]{:T(128)} %constant.8.clone.1), dimensions={2,4}, to_apply=%region_0.1 | reduce | flops 393216 | bytes 2359300 | tf_op jit(solution)/shard_map/reduce_sum | solution.py:99
  70.0 255.0 %all-reduce.5.cloned.1.call-done = (f32[3,3,256,256]{3,2,1,0:T(8,128)}, f32[3,256,256]{2,1,0:T(8,128)}) async-done(((f32[3,3,256,256]{3,2,1,0:T(8,128)}, f32[3,256,256]{2,1,0:T(8,128)}), (f32[3,3,256,256]{3,2,1,0:T(8,128)}, f32[3,256,256]{2,1,0:T(8,128)})) %all-reduce.5.cloned.1.call-update) | async-done | bytes 3145744 | tf_op jit(solution)/shard_map/psum | solution.py:101
  325.0 3.3 copy.18
  328.3 0.9 copy.19
  (62 shorter events, 17.8 us)
Async XLA Ops:
  7.2 317.8 %all-reduce.5.cloned.1.call-start = ((), (), s32[]{:S(2)}) async-start(), calls=%async_computation | async-start | bytes 6291456 | tf_op jit(solution)/shard_map/psum | solution.py:101
  8.1 13.2 %collective-permute-start = (bf16[4,1,32,256]{3,2,1,0:T(8,128)(2,1)S(1)}, bf16[4,1,32,256]{3,2,1,0:T(8,128)(2,1)S(1)}, u32[]{:S(2)}, u32[]{:S(2)}) collective-permute-start(bf16[4,1,32,256]{3,2,1,0:T(8,128)(2,1)S(1)} %get-tuple-element.29), channel_id=1, source_target_pairs={{0,1},{1,2},{2,3},{3,4},{4,5},{5,6},{6,7},{8,9},{9,10},{10,11},{11... | collective-permute-start | bytes 196616 | tf_op jit(solution)/shard_map/ppermute | solution.py:12
  13.0 8.3 %copy-start.6 = (bf16[1,4,4,32,256]{4,3,2,1,0:T(8,128)(2,1)S(1)}, bf16[1,4,4,32,256]{4,3,2,1,0:T(8,128)(2,1)}, u32[]{:S(2)}) copy-start(bf16[1,4,4,32,256]{4,3,2,1,0:T(8,128)(2,1)} %param.4) | copy-start | bytes 786436
  13.0 8.3 %collective-permute-start.1 = (bf16[4,1,32,256]{3,2,1,0:T(8,128)(2,1)S(1)}, bf16[4,1,32,256]{3,2,1,0:T(8,128)(2,1)S(1)}, u32[]{:S(2)}, u32[]{:S(2)}) collective-permute-start(bf16[4,1,32,256]{3,2,1,0:T(8,128)(2,1)S(1)} %get-tuple-element.30), channel_id=1, source_target_pairs={{1,0},{2,1},{3,2},{4,3},{5,4},{6,5},{7,6},{9,8},{10,9},{11,10},{12... | collective-permute-start | bytes 196616 | tf_op jit(solution)/shard_map/ppermute | solution.py:15
  17.0 20.6 %collective-permute-start.3 = (bf16[2,8,64,256]{3,2,1,0:T(8,128)(2,1)}, bf16[2,8,64,256]{3,2,1,0:T(8,128)(2,1)}, u32[]{:S(2)}, u32[]{:S(2)}) collective-permute-start(bf16[2,8,64,256]{3,2,1,0:T(8,128)(2,1)} %slice_bitcast_fusion), channel_id=1, source_target_pairs={{8,0},{16,8},{24,16},{9,1},{17,9},{25,17},{10,2},{18,10},{26,18},{... | collective-permute-start | bytes 1572872 | tf_op jit(solution)/shard_map/ppermute | solution.py:23
  24.0 4.2 %copy-start.2 = (bf16[3,3,256,256]{3,2,1,0:T(8,128)(2,1)S(1)}, bf16[3,3,256,256]{3,2,1,0:T(8,128)(2,1)}, u32[]{:S(2)}) copy-start(bf16[3,3,256,256]{3,2,1,0:T(8,128)(2,1)} %param.5) | copy-start | bytes 3538948
  31.7 5.0 %copy-start = (bf16[1,4,8,64,256]{4,3,2,1,0:T(8,128)(2,1)S(1)}, bf16[1,4,8,64,256]{4,3,2,1,0:T(8,128)(2,1)}, u32[]{:S(2)}) copy-start(bf16[1,4,8,64,256]{4,3,2,1,0:T(8,128)(2,1)} %param.7) | copy-start | bytes 3145732
  32.5 4.7 %copy-start.4 = (bf16[3,256,256]{2,1,0:T(8,128)(2,1)S(1)}, bf16[3,256,256]{2,1,0:T(8,128)(2,1)}, u32[]{:S(2)}) copy-start(bf16[3,256,256]{2,1,0:T(8,128)(2,1)} %param.6) | copy-start | bytes 1179652
  32.5 20.0 %collective-permute-start.2 = (bf16[2,8,64,256]{3,2,1,0:T(8,128)(2,1)S(1)}, bf16[2,8,64,256]{3,2,1,0:T(8,128)(2,1)S(1)}, u32[]{:S(2)}, u32[]{:S(2)}) collective-permute-start(bf16[2,8,64,256]{3,2,1,0:T(8,128)(2,1)S(1)} %bitcast.235), channel_id=1, source_target_pairs={{0,8},{8,16},{16,24},{1,9},{9,17},{17,25},{2,10},{10,18},{18,26},{... | collective-permute-start | bytes 1572872 | tf_op jit(solution)/shard_map/ppermute | solution.py:23
  37.6 1.8 copy-start.1
  42.2 15.0 %collective-permute-start.4 = (bf16[4,1,64,256]{3,2,1,0:T(8,128)(2,1)}, bf16[4,1,64,256]{3,2,1,0:T(8,128)(2,1)S(1)}, u32[]{:S(2)}, u32[]{:S(2)}) collective-permute-start(bf16[4,1,64,256]{3,2,1,0:T(8,128)(2,1)} %get-tuple-element.27), channel_id=1, source_target_pairs={{0,1},{1,2},{2,3},{3,4},{4,5},{5,6},{6,7},{8,9},{9,10},{10,11},{11... | collective-permute-start | bytes 393224 | tf_op jit(solution)/shard_map/ppermute | solution.py:12
  46.4 10.8 %collective-permute-start.5 = (bf16[4,1,64,256]{3,2,1,0:T(8,128)(2,1)}, bf16[4,1,64,256]{3,2,1,0:T(8,128)(2,1)S(1)}, u32[]{:S(2)}, u32[]{:S(2)}) collective-permute-start(bf16[4,1,64,256]{3,2,1,0:T(8,128)(2,1)} %get-tuple-element.28), channel_id=1, source_target_pairs={{1,0},{2,1},{3,2},{4,3},{5,4},{6,5},{7,6},{9,8},{10,9},{11,10},{12... | collective-permute-start | bytes 393224 | tf_op jit(solution)/shard_map/ppermute | solution.py:15
  52.5 1.4 copy-start.3
  325.0 3.3 copy-start.5
Sparse Core Ops, SparseCore 0:
  57.3 267.6 all-reduce.4
where the time goes:
time: 337 us; the launch traced here: 336 us
  waiting for transfers between devices  255 us (76%)
  matrix products  21.2 us (6%)
  local copies, waits for them, and re-layouts  19.1 us (6%)
  starting transfers between devices  18.7 us (6%)
  between operations  14.5 us (4%)
  other arithmetic  7.5 us (2%)
    psum x1, waiting for transfers between devices, on_device(): lax.psum((spatial_grad, temporal_grad), ('dp', 'tm', 'height'))  255 us
    ppermute x2, starting transfers between devices, extended(): lax.ppermute(lax.slice_in_dim(block, block.shape[dim] - width, None, axis...  9.1 us
  transfers between devices with their start and end apart: 7, of which 1 were waited for; matrix products, arithmetic and copies ran while one was open for 12% of the time, Pallas kernels for 0%

commit v1 on v0

--- a/solution.py
+++ b/solution.py
@@ -2,6 +2,187 @@
 import jax.numpy as jnp
 from jax import lax
 from jax.sharding import PartitionSpec as P
+from jax.experimental import pallas as pl
+from jax.experimental.pallas import tpu as pltpu
+
+F32 = jnp.float32
+BF16 = jnp.bfloat16
+MESH = pl.DeviceIdType.MESH
+N0, N1, N2, N3 = 192, 24, 6, 3
+
+
+def place():
+    dp, tm, h = lax.axis_index("dp"), lax.axis_index("tm"), lax.axis_index("height")
+    return dict(x=tm, y=dp // 2, z=(dp % 2) * 4 + h // 2, c=h % 2)
+
+
+def device(p):
+    return (p["y"] * 2 + p["z"] // 4, p["x"], (p["z"] % 4) * 2 + p["c"])
+
+
+SIZE = dict(x=4, y=4, z=8, c=2)
+
+
+def peer(me, axis, d):
+    return {**me, axis: (me[axis] + d) % SIZE[axis]}
+
+
+def partners(me):
+    return [peer(me, axis, d) for axis in ("c", "x", "y", "z") for d in range(1, SIZE[axis])]
+
+
+AR_SCRATCH = [
+    pltpu.VMEM((N0, 8, 256), F32),
+    pltpu.VMEM((N0, 8, 256), F32),
+    pltpu.VMEM((N0, 8, 256), BF16),
+    pltpu.VMEM((2, 3, N1, 8, 256), BF16),
+    pltpu.VMEM((2, N1, 8, 256), F32),
+    pltpu.VMEM((2, 3, N2, 8, 256), F32),
+    pltpu.VMEM((2, N2, 8, 256), F32),
+    pltpu.VMEM((7, N3, 8, 128), F32),
+    pltpu.VMEM((2 * N0, 8, 256), BF16),
+    pltpu.SemaphoreType.DMA((40,)),
+    pltpu.SemaphoreType.DMA((40,)),
+]
+
+
+def loop(count, body):
+    def step(i, carry):
+        body(i)
+        return carry
+
+    lax.fori_loop(0, count, step, 0)
+
+
+def ar_kernel(x_ref, s_out, t_out, recv0, acc, snd1, recv1, acc1, recv2, acc2, recv3, full, ssem, rsem):
+    me = place()
+    barrier = pltpu.get_barrier_semaphore()
+    others = partners(me)
+    for p in others:
+        pl.semaphore_signal(barrier, inc=1, device_id=device(p), device_id_type=MESH)
+    pl.semaphore_wait(barrier, len(others))
+    used = [0]
+
+    def send(src, dst, to):
+        k = used[0]
+        used[0] += 1
+        copy = pltpu.make_async_remote_copy(
+            src_ref=src, dst_ref=dst, send_sem=ssem.at[k], recv_sem=rsem.at[k],
+            device_id=device(to), device_id_type=MESH,
+        )
+        copy.start()
+        return copy
+
+    started = []
+
+    def exchange(copies):
+        started.extend(copies)
+        for c in copies:
+            c.wait_recv()
+
+    c = me["c"]
+    exchange([send(x_ref.at[pl.ds((1 - c) * N0, N0)], recv0, peer(me, "c", 1))])
+
+    def add0(i):
+        at = pl.ds(i * 12, 12)
+        total = x_ref[pl.ds(c * N0 + i * 12, 12)] + recv0[at]
+        acc[at] = total
+        snd1[at] = total.astype(BF16)
+
+    loop(16, add0)
+    order = (("x", "y"), ("y", "x"))
+    copies = []
+    for part in range(2):
+        axis = order[part][0]
+        for d in range(1, 4):
+            to = peer(me, axis, d)
+            copies.append(send(snd1.at[pl.ds(part * 96 + to[axis] * N1, N1)], recv1.at[part, d - 1], to))
+    exchange(copies)
+    for part in range(2):
+        mine = part * 96 + me[order[part][0]] * N1
+
+        def add1(i, part=part, mine=mine):
+            at = pl.ds(i * 6, 6)
+            total = acc[pl.ds(mine + i * 6, 6)]
+            for d in range(3):
+                total = total + recv1[part, d, at].astype(F32)
+            acc1[part, at] = total
+
+        loop(4, add1)
+    copies = []
+    for part in range(2):
+        axis = order[part][1]
+        for d in range(1, 4):
+            to = peer(me, axis, d)
+            copies.append(send(acc1.at[part, pl.ds(to[axis] * N2, N2)], recv2.at[part, d - 1], to))
+    exchange(copies)
+    for part in range(2):
+        total = acc1[part, pl.ds(me[order[part][1]] * N2, N2)]
+        for d in range(3):
+            total = total + recv2[part, d]
+        acc2[part] = total
+
+    def zslice(z):
+        return pl.ds((z % 4) // 2 * N3, N3), slice(None), pl.ds(pl.multiple_of((z % 2) * 128, 128), 128)
+
+    copies = []
+    for d in range(1, 8):
+        to = peer(me, "z", d)
+        copies.append(send(acc2.at[(to["z"] // 4, *zslice(to["z"]))], recv3.at[d - 1], to))
+    exchange(copies)
+    z = me["z"]
+    total = acc2[(z // 4, *zslice(z))]
+    for d in range(7):
+        total = total + recv3[d]
+    part = z // 4
+    first = (me["x"] * (1 - part) + me["y"] * part) * N1
+    second = (me["y"] * (1 - part) + me["x"] * part) * N2
+    base = c * N0 + part * 96 + first + second
+    rows, _, lanes = zslice(z)
+    shard = (pl.ds(base + (z % 4) // 2 * N3, N3), slice(None), lanes)
+    full[shard] = total.astype(BF16)
+    exchange([send(full.at[shard], full.at[shard], peer(me, "z", d)) for d in range(1, 8)])
+    copies = []
+    for part in range(2):
+        a, b = order[part]
+        at = pl.ds(c * N0 + part * 96 + me[a] * N1 + me[b] * N2, N2)
+        for d in range(1, 4):
+            copies.append(send(full.at[at], full.at[at], peer(me, b, d)))
+    exchange(copies)
+    copies = []
+    for part in range(2):
+        a, b = order[part]
+        at = pl.ds(c * N0 + part * 96 + me[a] * N1, N1)
+        for d in range(1, 4):
+            copies.append(send(full.at[at], full.at[at], peer(me, a, d)))
+    exchange(copies)
+    at = pl.ds(c * N0, N0)
+    exchange([send(full.at[at], full.at[at], peer(me, "c", 1))])
+
+    def spread(i):
+        s_out[pl.ds(i * 12, 12)] = full[pl.ds(i * 12, 12)].astype(F32)
+
+    def spread_t(i):
+        t_out[pl.ds(i * 12, 12)] = full[pl.ds(288 + i * 12, 12)].astype(F32)
+
+    loop(24, spread)
+    loop(8, spread_t)
+    for copy in started:
+        copy.wait_send()
+
+
+def all_reduce(x):
+    return pl.pallas_call(
+        ar_kernel,
+        out_shape=(jax.ShapeDtypeStruct((288, 8, 256), F32), jax.ShapeDtypeStruct((96, 8, 256), F32)),
+        in_specs=[pl.BlockSpec(memory_space=pltpu.VMEM)],
+        out_specs=(pl.BlockSpec(memory_space=pltpu.VMEM), pl.BlockSpec(memory_space=pltpu.VMEM)),
+        scratch_shapes=AR_SCRATCH,
+        compiler_params=pltpu.CompilerParams(
+            collective_id=0, has_side_effects=True, vmem_limit_bytes=40 << 20
+        ),
+        name="all_reduce",
+    )(x)
 
 
 def extended(block, sides, width):
@@ -98,7 +279,10 @@
     input_grad = (
         total.reshape(frames, rows_low, 2, cols_low, 2, chan).sum(axis=(2, 4)).astype(jnp.bfloat16)
     )
-    spatial_grad, temporal_grad = lax.psum((spatial_grad, temporal_grad), ("dp", "tm", "height"))
+    both = jnp.concatenate([spatial_grad.reshape(9, chan, chan), temporal_grad], 0)
+    spatial_grad, temporal_grad = all_reduce(both.reshape(384, 8, chan))
+    spatial_grad = spatial_grad.reshape(3, 3, chan, chan)
+    temporal_grad = temporal_grad.reshape(3, chan, chan)
     return (section_out, input_grad[None], spatial_grad, temporal_grad)
 
 

time: 337 us -> 115 us (0.34)
  waiting for transfers between devices: 255 us -> 0.02 us
  Pallas kernels: 0 us -> 48.9 us
  between operations: 14.5 us -> 1.09 us
    psum x1 -> x0, waiting for transfers between devices: 255 us -> none  [on_device(): lax.psum((spatial_grad, temporal_grad), ('dp', 'tm', 'height'))]
    pallas_call x0 -> x1, Pallas kernels: none -> 48.9 us  [all_reduce(): pl.pallas_call(ar_kernel, out_shape=(jax.ShapeDtypeStruct((288, 8, 256),...]
  transfers between devices with their start and end apart: 7 -> 6, of which waited for: 1 -> 0; matrix products, arithmetic and copies ran while one was open for 12% -> 24% of each run, Pallas kernels for 0% -> 43%
where the time goes in v1:
time: 115 us
  Pallas kernels  48.9 us (43%)
  matrix products  22.5 us (20%)
  starting transfers between devices  19 us (17%)
  local copies, waits for them, and re-layouts  16.6 us (14%)
  other arithmetic  6.59 us (6%)
    pallas_call x1, Pallas kernels, all_reduce(): pl.pallas_call(ar_kernel, out_shape=(jax.ShapeDtypeStruct((288, 8, 256),...  48.9 us
    ppermute x2, starting transfers between devices, extended(): lax.ppermute(lax.slice_in_dim(block, block.shape[dim] - width, None, axis...  9.14 us
    ppermute x2, starting transfers between devices, shifted(): return lax.ppermute(block, axis, route)  5.61 us
    dot_general x9, matrix products, on_device(): jnp.dot(piece, spatial_weight[i, j].T, preferred_element_type=jnp.float32)  5.58 us
    slice x2, local copies, waits for them, and re-layouts, spatial_apply(): piece = padded[:, i:i + rows, j:j + cols, :].reshape(-1, chan)  4.54 us
    dot_general x3, matrix products, on_device(): jnp.dot(grad_ext[k:k + frames].reshape(-1, chan), temporal_weight[k].T, p...  4.53 us
    dot_general x9, matrix products, on_device(): lax.dot_general(piece, pre_grad, (((0,), (0,)), ((), ())), preferred_elem...  4.39 us
    dot_general x9, matrix products, spatial_apply(): jnp.dot(piece, weights[i, j], preferred_element_type=jnp.float32)  4.25 us
  transfers between devices with their start and end apart: 6, of which 0 were waited for; matrix products, arithmetic and copies ran while one was open for 24% of the time, Pallas kernels for 43%

profile of v1, /device:TPU:1, one launch (start us, length us, event | category | flops | bytes accessed | tf_op | source)
XLA Modules:
  0.0 114.6 jit_solution(9156022470295666778)
XLA Ops:
  0.6 0.9 fusion.80
  1.5 4.9 %collective-permute-start = (bf16[4,1,32,256]{3,2,1,0:T(8,128)(2,1)S(1)}, bf16[4,1,32,256]{3,2,1,0:T(8,128)(2,1)S(1)}, u32[]{:S(2)}, u32[]{:S(2)}) collective-permute-start(bf16[4,1,32,256]{3,2,1,0:T(8,128)(2,1)S(1)} %get-tuple-element.31), channel_id=1, source_target_pairs={{0,1},{1,2},{2,3},{3,4},{4,5},{5,6},{6,7},{8,9},{9,10},{10,11},{11... | collective-permute-start | bytes 196616 | tf_op jit(solution)/shard_map/ppermute | solution.py:193
  6.5 2.1 %collective-permute-start.1 = (bf16[4,1,32,256]{3,2,1,0:T(8,128)(2,1)S(1)}, bf16[4,1,32,256]{3,2,1,0:T(8,128)(2,1)S(1)}, u32[]{:S(2)}, u32[]{:S(2)}) collective-permute-start(bf16[4,1,32,256]{3,2,1,0:T(8,128)(2,1)S(1)} %get-tuple-element.32), channel_id=1, source_target_pairs={{1,0},{2,1},{3,2},{4,3},{5,4},{6,5},{7,6},{9,8},{10,9},{11,10},{12... | collective-permute-start | bytes 196616 | tf_op jit(solution)/shard_map/ppermute | solution.py:196
  8.5 1.9 %slice_bitcast_fusion = bf16[2,8,64,256]{3,2,1,0:T(8,128)(2,1)} fusion(bf16[1,4,8,64,256]{4,3,2,1,0:T(8,128)(2,1)} %param.7), kind=kLoop, calls=%fused_computation.75 | loop fusion | bytes 1048576 | tf_op jit(solution)/shard_map/slice | solution.py:238
  10.4 1.3 %collective-permute-start.3 = (bf16[2,8,64,256]{3,2,1,0:T(8,128)(2,1)}, bf16[2,8,64,256]{3,2,1,0:T(8,128)(2,1)}, u32[]{:S(2)}, u32[]{:S(2)}) collective-permute-start(bf16[2,8,64,256]{3,2,1,0:T(8,128)(2,1)} %slice_bitcast_fusion), channel_id=1, source_target_pairs={{8,0},{16,8},{24,16},{9,1},{17,9},{25,17},{10,2},{18,10},{26,18},{... | collective-permute-start | bytes 1572872 | tf_op jit(solution)/shard_map/ppermute | solution.py:204
  11.7 3.0 %fusion.29 = f32[2048,256]{1,0:T(8,128)} fusion(bf16[2048,256]{1,0:T(8,128)(2,1)} %bitcast.201, bf16[3,256,256]{2,1,0:T(8,128)(2,1)} %param.6), kind=kOutput, calls=%fused_computation.82 | convolution fusion | flops 268435456 | bytes 3276800 | tf_op jit(solution)/shard_map/dot_general | solution.py:244
  14.9 1.4 %broadcast_in_dim.8 = bf16[4,12,32,2,256]{4,3,2,1,0:T(2,128)(2,1)S(1)} broadcast(bf16[4,12,32,256]{3,2,1,0:T(8,128)(2,1)S(1)} %bitcast.240), dimensions={0,1,2,4} | broadcast | bytes 2359296 | tf_op jit(solution)/shard_map/broadcast_in_dim | solution.py:224
  16.2 0.6 reshape.123
  17.4 4.2 %pad_slice_fusion.4 = (bf16[4,8,64,256]{3,2,1,0:T(8,128)(2,1)S(1)}, bf16[4,8,64,256]{3,2,1,0:T(8,128)(2,1)S(1)}, bf16[4,8,64,256]{3,2,1,0:T(8,128)(2,1)S(1)}, bf...) fusion(bf16[4,10,64,256]{3,2,1,0:T(8,128)(2,1)S(1)} %slice.207), kind=kLoop, calls=%fused_computation.69 | loop fusion | bytes 7602176 | tf_op jit(solution)/shard_map/slice | solution.py:212
  25.1 0.8 multiply_convert_fusion
  25.9 4.3 %collective-permute-start.2 = (bf16[2,8,64,256]{3,2,1,0:T(8,128)(2,1)S(1)}, bf16[2,8,64,256]{3,2,1,0:T(8,128)(2,1)S(1)}, u32[]{:S(2)}, u32[]{:S(2)}) collective-permute-start(bf16[2,8,64,256]{3,2,1,0:T(8,128)(2,1)S(1)} %bitcast.245), channel_id=1, source_target_pairs={{0,8},{8,16},{16,24},{1,9},{9,17},{17,25},{2,10},{10,18},{18,26},{... | collective-permute-start | bytes 1572872 | tf_op jit(solution)/shard_map/ppermute | solution.py:204
  30.8 1.4 %pad_maximum_fusion.2 = (bf16[4,8,64,256]{3,2,1,0:T(8,128)(2,1)S(1)}, bf16[4,8,64,256]{3,2,1,0:T(8,128)(2,1)S(1)}) fusion(bf16[2,8,64,256]{3,2,1,0:T(8,128)(2,1)} %collective-permute-done.3, bf16[4,8,64,256]{3,2,1,0:T(8,128)(2,1)S(1)} %bitcast.202), kind=kLoop, calls=%fused_computation.67 | loop fusion | flops 1048576 | bytes 3670016 | tf_op jit(solution)/shard_map/concatenate | solution.py:239
  33.0 1.1 fusion.4
  38.1 4.2 %collective-permute-start.4 = (bf16[4,1,64,256]{3,2,1,0:T(8,128)(2,1)S(1)}, bf16[4,1,64,256]{3,2,1,0:T(8,128)(2,1)S(1)}, u32[]{:S(2)}, u32[]{:S(2)}) collective-permute-start(bf16[4,1,64,256]{3,2,1,0:T(8,128)(2,1)S(1)} %get-tuple-element.29), channel_id=1, source_target_pairs={{0,1},{1,2},{2,3},{3,4},{4,5},{5,6},{6,7},{8,9},{9,10},{10,11},{11... | collective-permute-start | bytes 393224 | tf_op jit(solution)/shard_map/ppermute | solution.py:193
  42.3 2.1 %collective-permute-start.5 = (bf16[4,1,64,256]{3,2,1,0:T(8,128)(2,1)S(1)}, bf16[4,1,64,256]{3,2,1,0:T(8,128)(2,1)S(1)}, u32[]{:S(2)}, u32[]{:S(2)}) collective-permute-start(bf16[4,1,64,256]{3,2,1,0:T(8,128)(2,1)S(1)} %get-tuple-element.30), channel_id=1, source_target_pairs={{1,0},{2,1},{3,2},{4,3},{5,4},{6,5},{7,6},{9,8},{10,9},{11,10},{12... | collective-permute-start | bytes 393224 | tf_op jit(solution)/shard_map/ppermute | solution.py:196
  46.6 1.4 %fusion.5 = bf16[2048,256]{1,0:T(8,128)(2,1)} fusion(f32[2048,256]{1,0:T(8,128)S(1)} %convolution_add_fusion.10, bf16[2048,256]{1,0:T(8,128)(2,1)S(1)} %bitcast.211, bf16[3,256,256]{2,1,0:T(8,128)(2,1)S(1)} %copy-done.3), kind=kOutput, calls=%fused_computation.27 | convolution fusion | flops 269484032 | bytes 4325376 | tf_op jit(solution)/shard_map/dot_general | solution.py:232
  48.5 48.9 %all_reduce.1 = (f32[288,8,256]{2,1,0:T(8,128)S(1)}, f32[96,8,256]{2,1,0:T(8,128)S(1)}) custom-call(f32[384,8,256]{2,1,0:T(8,128)S(1)} %bitcast.195), custom_call_target="tpu_custom_call" | custom-call | tf_op jit(solution)/shard_map/all_reduce/pallas_call | solution.py:175
  97.4 0.8 fusion.10
  98.2 0.9 fusion.78
  103.0 1.9 %fusion.1 = f32[2048,256]{1,0:T(8,128)} fusion(f32[2048,256]{1,0:T(8,128)S(1)} %fusion.32, f32[2048,256]{1,0:T(8,128)S(1)} %convolution_add_fusion.1, bf16[2048,256]{1,0:T(8,128)(2,1)S(1)} %bitcast.231, bf16[3,3,256,256]{3,2,1,0:T(8,128)(2,1)S(1)} %copy-done.2), kind=kOutput, calls=%fused_computation.4 | convolution fusion | flops 269484032 | bytes 7471104 | tf_op jit(solution)/shard_map/dot_general | solution.py:276
  104.9 3.5 %reshape.148 = f32[4,4,2,32,2,256]{5,4,3,2,1,0:T(2,128)} reshape(f32[2048,256]{1,0:T(8,128)} %fusion.1) | data formatting | bytes 4194304 | tf_op jit(solution)/shard_map/reshape | solution.py:280
  108.4 4.0 %reduce_sum.9 = bf16[4,4,32,256]{3,2,1,0:T(8,128)(2,1)} reduce(f32[4,4,2,32,2,256]{5,4,3,2,1,0:T(2,128)} %reshape.148, f32[]{:T(128)} %constant.8.clone.1), dimensions={2,4}, to_apply=%region_0.1 | reduce | flops 393216 | bytes 2359300 | tf_op jit(solution)/shard_map/reduce_sum | solution.py:280
  112.3 1.4 %copy.21 = f32[3,3,256,256]{3,2,1,0:T(8,128)} copy(f32[3,3,256,256]{3,2,1,0:T(8,128)S(1)} %bitcast.196) | data formatting | bytes 4718592
  113.7 0.9 copy.22
  (55 shorter events, 15.8 us)
Async XLA Ops:
  1.5 13.2 %collective-permute-start = (bf16[4,1,32,256]{3,2,1,0:T(8,128)(2,1)S(1)}, bf16[4,1,32,256]{3,2,1,0:T(8,128)(2,1)S(1)}, u32[]{:S(2)}, u32[]{:S(2)}) collective-permute-start(bf16[4,1,32,256]{3,2,1,0:T(8,128)(2,1)S(1)} %get-tuple-element.31), channel_id=1, source_target_pairs={{0,1},{1,2},{2,3},{3,4},{4,5},{5,6},{6,7},{8,9},{9,10},{10,11},{11... | collective-permute-start | bytes 196616 | tf_op jit(solution)/shard_map/ppermute | solution.py:193
  6.5 8.3 %copy-start.4 = (bf16[1,4,4,32,256]{4,3,2,1,0:T(8,128)(2,1)S(1)}, bf16[1,4,4,32,256]{4,3,2,1,0:T(8,128)(2,1)}, u32[]{:S(2)}) copy-start(bf16[1,4,4,32,256]{4,3,2,1,0:T(8,128)(2,1)} %param.4) | copy-start | bytes 786436
  6.5 8.2 %collective-permute-start.1 = (bf16[4,1,32,256]{3,2,1,0:T(8,128)(2,1)S(1)}, bf16[4,1,32,256]{3,2,1,0:T(8,128)(2,1)S(1)}, u32[]{:S(2)}, u32[]{:S(2)}) collective-permute-start(bf16[4,1,32,256]{3,2,1,0:T(8,128)(2,1)S(1)} %get-tuple-element.32), channel_id=1, source_target_pairs={{1,0},{2,1},{3,2},{4,3},{5,4},{6,5},{7,6},{9,8},{10,9},{11,10},{12... | collective-permute-start | bytes 196616 | tf_op jit(solution)/shard_map/ppermute | solution.py:196
  10.4 20.3 %collective-permute-start.3 = (bf16[2,8,64,256]{3,2,1,0:T(8,128)(2,1)}, bf16[2,8,64,256]{3,2,1,0:T(8,128)(2,1)}, u32[]{:S(2)}, u32[]{:S(2)}) collective-permute-start(bf16[2,8,64,256]{3,2,1,0:T(8,128)(2,1)} %slice_bitcast_fusion), channel_id=1, source_target_pairs={{8,0},{16,8},{24,16},{9,1},{17,9},{25,17},{10,2},{18,10},{26,18},{... | collective-permute-start | bytes 1572872 | tf_op jit(solution)/shard_map/ppermute | solution.py:204
  17.4 4.2 %copy-start.2 = (bf16[3,3,256,256]{3,2,1,0:T(8,128)(2,1)S(1)}, bf16[3,3,256,256]{3,2,1,0:T(8,128)(2,1)}, u32[]{:S(2)}) copy-start(bf16[3,3,256,256]{3,2,1,0:T(8,128)(2,1)} %param.5) | copy-start | bytes 3538948
  25.1 5.2 %copy-start.3 = (bf16[3,256,256]{2,1,0:T(8,128)(2,1)S(1)}, bf16[3,256,256]{2,1,0:T(8,128)(2,1)}, u32[]{:S(2)}) copy-start(bf16[3,256,256]{2,1,0:T(8,128)(2,1)} %param.6) | copy-start | bytes 1179652
  25.9 4.8 %copy-start = (bf16[1,4,8,64,256]{4,3,2,1,0:T(8,128)(2,1)S(1)}, bf16[1,4,8,64,256]{4,3,2,1,0:T(8,128)(2,1)}, u32[]{:S(2)}) copy-start(bf16[1,4,8,64,256]{4,3,2,1,0:T(8,128)(2,1)} %param.7) | copy-start | bytes 3145732
  25.9 19.5 %collective-permute-start.2 = (bf16[2,8,64,256]{3,2,1,0:T(8,128)(2,1)S(1)}, bf16[2,8,64,256]{3,2,1,0:T(8,128)(2,1)S(1)}, u32[]{:S(2)}, u32[]{:S(2)}) collective-permute-start(bf16[2,8,64,256]{3,2,1,0:T(8,128)(2,1)S(1)} %bitcast.245), channel_id=1, source_target_pairs={{0,8},{8,16},{16,24},{1,9},{9,17},{17,25},{2,10},{10,18},{18,26},{... | collective-permute-start | bytes 1572872 | tf_op jit(solution)/shard_map/ppermute | solution.py:204
  30.7 1.8 %copy-start.1 = (f32[2048,256]{1,0:T(8,128)S(1)}, f32[2048,256]{1,0:T(8,128)}, u32[]{:S(2)}) copy-start(f32[2048,256]{1,0:T(8,128)} %fusion.29) | copy-start | bytes 6291460
  38.1 59.3 %collective-permute-start.4 = (bf16[4,1,64,256]{3,2,1,0:T(8,128)(2,1)S(1)}, bf16[4,1,64,256]{3,2,1,0:T(8,128)(2,1)S(1)}, u32[]{:S(2)}, u32[]{:S(2)}) collective-permute-start(bf16[4,1,64,256]{3,2,1,0:T(8,128)(2,1)S(1)} %get-tuple-element.29), channel_id=1, source_target_pairs={{0,1},{1,2},{2,3},{3,4},{4,5},{5,6},{6,7},{8,9},{9,10},{10,11},{11... | collective-permute-start | bytes 393224 | tf_op jit(solution)/shard_map/ppermute | solution.py:193
  42.3 55.1 %collective-permute-start.5 = (bf16[4,1,64,256]{3,2,1,0:T(8,128)(2,1)S(1)}, bf16[4,1,64,256]{3,2,1,0:T(8,128)(2,1)S(1)}, u32[]{:S(2)}, u32[]{:S(2)}) collective-permute-start(bf16[4,1,64,256]{3,2,1,0:T(8,128)(2,1)S(1)} %get-tuple-element.30), channel_id=1, source_target_pairs={{1,0},{2,1},{3,2},{4,3},{5,4},{6,5},{7,6},{9,8},{10,9},{11,10},{12... | collective-permute-start | bytes 393224 | tf_op jit(solution)/shard_map/ppermute | solution.py:196

commit v2 on v1

v2 whole, which is shorter than its diff:
```python
import jax
import jax.numpy as jnp
from jax import lax
from jax.experimental import pallas as pl
from jax.experimental.pallas import tpu as pltpu
from jax.sharding import PartitionSpec as P

F32 = jnp.float32
BF16 = jnp.bfloat16
MESH = pl.DeviceIdType.MESH
N0, N1, N2, N3 = 192, 24, 6, 3
SIZE = dict(x=4, y=4, z=8, c=2)


def place():
    dp, tm, h = lax.axis_index("dp"), lax.axis_index("tm"), lax.axis_index("height")
    return dict(x=tm, y=dp // 2, z=(dp % 2) * 4 + h // 2, c=h % 2)


def device(p):
    return (p["y"] * 2 + p["z"] // 4, p["x"], (p["z"] % 4) * 2 + p["c"])


def peer(me, axis, d):
    return {**me, axis: (me[axis] + d) % SIZE[axis]}


def loop(count, body):
    def step(i, carry):
        body(i)
        return carry

    lax.fori_loop(0, count, step, 0)


def nn(a, b):
    return lax.dot_general(a, b, (((1,), (0,)), ((), ())), preferred_element_type=F32)


def nt(a, b):
    return lax.dot_general(a, b, (((1,), (1,)), ((), ())), preferred_element_type=F32)


SCRATCH = dict(
    wv=pltpu.VMEM((9, 256, 256), BF16),
    tv=pltpu.VMEM((3, 256, 256), BF16),
    low=pltpu.VMEM((6, 6, 32, 256), BF16),
    cot=pltpu.VMEM((6, 8, 64, 256), BF16),
    cotp=pltpu.VMEM((6, 512, 256), BF16),
    tmp=pltpu.VMEM((16, 64, 128), F32),
    ys=pltpu.VMEM((9, 24, 32, 256), F32),
    act=pltpu.VMEM((6, 512, 256), BF16),
    actT=pltpu.VMEM((4, 256, 512), BF16),
    lowT0=pltpu.VMEM((256, 640), BF16),
    lowT1=pltpu.VMEM((256, 512), BF16),
    lowT2=pltpu.VMEM((256, 640), BF16),
    ds=pltpu.VMEM((4, 512, 256), F32),
    pg=pltpu.VMEM((4, 10, 64, 256), BF16),
    odd=pltpu.VMEM((3, 4, 5, 32, 256), BF16),
    even=pltpu.VMEM((3, 4, 4, 32, 256), BF16),
    grads=pltpu.VMEM((384, 8, 256), F32),
    so_v=pltpu.VMEM((4, 8, 64, 256), BF16),
    ig_acc=pltpu.VMEM((512, 256), F32),
    ig_v=pltpu.VMEM((4, 4, 32, 256), BF16),
    fin=pltpu.VMEM((384, 8, 256), F32),
    recv0=pltpu.VMEM((N0, 8, 256), F32),
    acc=pltpu.VMEM((N0, 8, 256), F32),
    snd1=pltpu.VMEM((N0, 8, 256), BF16),
    recv1=pltpu.VMEM((2, 3, N1, 8, 256), BF16),
    acc1=pltpu.VMEM((2, N1, 8, 256), F32),
    recv2=pltpu.VMEM((2, 3, N2, 8, 256), F32),
    acc2=pltpu.VMEM((2, N2, 8, 256), F32),
    recv3=pltpu.VMEM((7, N3, 8, 128), F32),
    full=pltpu.VMEM((2 * N0, 8, 256), BF16),
    ssem=pltpu.SemaphoreType.DMA((49,)),
    rsem=pltpu.SemaphoreType.DMA((49,)),
    lsem=pltpu.SemaphoreType.DMA((24,)),
)


def kernel(low_hbm, w_hbm, t_hbm, cot_hbm, so_hbm, ig_hbm, s_hbm, tg_hbm, *scratch):
    s = dict(zip(SCRATCH, scratch))
    low, cot, cotp, ys, act, ds, pg = (s[n] for n in ("low", "cot", "cotp", "ys", "act", "ds", "pg"))
    odd, even, grads, tmp, full = (s[n] for n in ("odd", "even", "grads", "tmp", "full"))
    wv, tv = s["wv"], s["tv"]
    me = place()
    dp, tm, h = lax.axis_index("dp"), lax.axis_index("tm"), lax.axis_index("height")
    yes = True
    barrier = pltpu.get_barrier_semaphore()
    others = [device(peer(me, axis, d)) for axis in ("c", "x", "y", "z") for d in range(1, SIZE[axis])]
    others += [(dp, (tm + i) % 4, (h + j) % 8) for i in (0, 1, 3) for j in (1, 7)]
    for to in others:
        pl.semaphore_signal(barrier, inc=1, device_id=to, device_id_type=MESH)

    local_used = [0]

    def local(src, dst):
        copy = pltpu.make_async_copy(src, dst, s["lsem"].at[local_used[0]])
        local_used[0] += 1
        copy.start()
        return copy

    load_low = local(low_hbm, low.at[pl.ds(2, 4), pl.ds(1, 4)])
    load_w = local(w_hbm, wv)
    load_cot = local(cot_hbm, cot.at[pl.ds(0, 4)])
    load_t = local(t_hbm, tv)

    @pl.when(tm == 0)
    def _():
        low[0:2] = jnp.zeros((2, 6, 32, 256), BF16)

    @pl.when(tm == 3)
    def _():
        cot[4:6] = jnp.zeros((2, 8, 64, 256), BF16)

    @pl.when(h == 0)
    def _():
        low[2:6, 0] = jnp.zeros((4, 32, 256), BF16)
        pg[:, 0] = jnp.zeros((4, 64, 256), BF16)

    @pl.when(h == 7)
    def _():
        low[2:6, 5] = jnp.zeros((4, 32, 256), BF16)
        pg[:, 9] = jnp.zeros((4, 64, 256), BF16)

    @pl.when((h == 0) & (tm > 0))
    def _():
        low[0:2, 0] = jnp.zeros((2, 32, 256), BF16)

    @pl.when((h == 7) & (tm > 0))
    def _():
        low[0:2, 5] = jnp.zeros((2, 32, 256), BF16)

    pl.semaphore_wait(barrier, len(others))
    used = [0]
    halos = []

    def halo(src, dst, to, sends, receives):
        k = used[0]
        used[0] += 1
        copy = pltpu.make_async_remote_copy(
            src_ref=src, dst_ref=dst, send_sem=s["ssem"].at[k], recv_sem=s["rsem"].at[k],
            device_id=to, device_id_type=MESH,
        )

        @pl.when(sends)
        def _():
            copy.start()

        halos.append((copy, sends))
        return copy, receives

    def arrive(pair):
        copy, receives = pair

        @pl.when(receives)
        def _():
            copy.wait_recv()

    up, down, right, left = (h + 1) % 8, (h + 7) % 8, (tm + 1) % 4, (tm + 3) % 4
    own, early = pl.ds(2, 4), pl.ds(0, 2)
    low_up = halo(low_hbm.at[:, 3], low.at[own, 0], (dp, tm, up), h < 7, h > 0)
    low_down = halo(low_hbm.at[:, 0], low.at[own, 5], (dp, tm, down), h > 0, h < 7)
    cots = [
        halo(cot_hbm.at[f], cot.at[4 + f], (dp, left, h), tm > 0, tm < 3) for f in range(2)
    ]
    last = pl.ds(2, 2)
    early_low = [
        halo(low_hbm.at[last], low.at[early, pl.ds(1, 4)], (dp, right, h), tm < 3, tm > 0),
        halo(low_hbm.at[last, 3], low.at[early, 0], (dp, right, up), (tm < 3) & (h < 7), (tm > 0) & (h > 0)),
        halo(low_hbm.at[last, 0], low.at[early, 5], (dp, right, down), (tm < 3) & (h > 0), (tm > 0) & (h < 7)),
    ]

    def split_columns(f):
        def row(y):
            for half in range(2):
                lanes = pl.ds(half * 128, 128)
                tmp[y * 2 + half] = cot[f, y, :, lanes].astype(F32)
                for b in range(2):
                    part = tmp[y * 2 + half, pl.ds(b, 32, stride=2), :]
                    cotp[f, pl.ds(y * 64 + b * 32, 32), lanes] = part.astype(BF16)

        loop(8, row)

    load_cot.wait()
    loop(4, split_columns)
    load_low.wait()
    load_w.wait()
    load_t.wait()
    arrive(low_up)
    arrive(low_down)
    col = lax.broadcasted_iota(jnp.int32, (32, 256), 0)

    def from_left(v):
        return jnp.where(col == 0, 0.0, pltpu.roll(v, 1, 0))

    def from_right(v):
        return jnp.where(col == 31, 0.0, pltpu.roll(v, 31, 0))

    def products(first, count):
        def one(ij):
            rows = low[pl.ds(first, count)].reshape(count * 192, 256)
            ys[ij, 0 : count * 6] = nn(rows, wv[ij]).reshape(count * 6, 32, 256)

        loop(9, one)

    def activate(first, count, slopes):
        def one(n):
            f, r = n // 4, n % 4
            at = f * 6 + r + 1
            for a in range(2):
                z = [ys[j, at - 1 + a] + ys[3 + j, at] + ys[6 + j, at + a] for j in range(3)]
                pres = (from_left(z[0]) + z[1] + z[2], z[0] + z[1] + from_right(z[2]))
                for b in range(2):
                    pre = pres[b]
                    sig = jax.nn.sigmoid(pre)
                    tokens = pl.ds((r * 2 + a) * 64 + b * 32, 32)
                    act[first + f, tokens] = (pre * sig).astype(BF16)
                    if slopes:
                        ds[f, tokens] = sig * (1.0 + pre * (1.0 - sig))

        loop(count * 4, one)

    products(2, 4)
    activate(2, 4, True)

    def flip(f):
        s["actT"][f] = act[2 + f].T

    loop(4, flip)
    s["lowT0"][...] = low[2:6, 0:5].reshape(640, 256).T
    s["lowT1"][...] = low[2:6, 1:5].reshape(512, 256).T
    s["lowT2"][...] = low[2:6, 1:6].reshape(640, 256).T

    def pre_grad(f):
        total = nt(cotp[f], tv[0]) + nt(cotp[f + 1], tv[1]) + nt(cotp[f + 2], tv[2])
        pg[f, 1:9] = (total * ds[f]).astype(BF16).reshape(8, 64, 256)

    loop(2, pre_grad)
    for pair in early_low:
        arrive(pair)
    products(0, 2)
    activate(0, 2, False)
    outs = []

    def section(t):
        total = nn(act[t + 2], tv[0]) + nn(act[t + 1], tv[1]) + nn(act[t], tv[2])
        for y in range(8):
            up_row = low[t + 2, y // 2 + 1].astype(F32)
            for b in range(2):
                at = y * 64 + b * 32
                value = total[at : at + 32] + up_row
                for half in range(2):
                    tmp[y * 2 + half, pl.ds(b, 32, stride=2), :] = value[:, half * 128 : half * 128 + 128]
        for y in range(8):
            for half in range(2):
                s["so_v"][t, y, :, half * 128 : half * 128 + 128] = tmp[y * 2 + half].astype(BF16)

    loop(4, section)
    outs.append(local(s["so_v"], so_hbm))

    for f in range(2):
        arrive(cots[f])
        split_columns(4 + f)
        pre_grad(2 + f)
    pg_up = halo(pg.at[:, 8], pg.at[:, 0], (dp, tm, up), h < 7, h > 0)
    pg_down = halo(pg.at[:, 1], pg.at[:, 9], (dp, tm, down), h > 0, h < 7)

    for k in range(3):
        total = nn(s["actT"][0], cotp[k])
        for f in range(1, 4):
            total = total + nn(s["actT"][f], cotp[f + k])
        grads[288 + 32 * k : 320 + 32 * k] = total.reshape(32, 8, 256)

    def put(ref, f, q, even_cols, odd_cols):
        ref[0, f, q] = (odd_cols + from_right(even_cols)).astype(BF16)
        ref[1, f, q] = (odd_cols + even_cols).astype(BF16)
        ref[2, f, q] = (from_left(odd_cols) + even_cols).astype(BF16)

    def rows_of(f, slots):
        halves = []
        for b in range(2):
            total = pg[f, slots[0], b * 32 : b * 32 + 32].astype(F32)
            for slot in slots[1:]:
                total = total + pg[f, slot, b * 32 : b * 32 + 32].astype(F32)
            halves.append(total)
        return halves

    def box(f):
        for q in range(5):
            slots = [n for n in (2 * q, 2 * q + 1) if 0 < n < 9]
            put(odd, f, q, *rows_of(f, slots))
        for r in range(4):
            put(even, f, r, *rows_of(f, (2 * r + 1, 2 * r + 2)))

    loop(4, box)

    def weight_grads(j):
        sums = odd[j].reshape(640, 256)
        grads[pl.ds(j * 32, 32)] = nn(s["lowT0"][...], sums).reshape(32, 8, 256)
        grads[pl.ds((6 + j) * 32, 32)] = nn(s["lowT2"][...], sums).reshape(32, 8, 256)
        grads[pl.ds((3 + j) * 32, 32)] = nn(s["lowT1"][...], even[j].reshape(512, 256)).reshape(32, 8, 256)

    loop(3, weight_grads)

    started = []

    def send(src, dst, to):
        k = used[0]
        used[0] += 1
        copy = pltpu.make_async_remote_copy(
            src_ref=src, dst_ref=dst, send_sem=s["ssem"].at[k], recv_sem=s["rsem"].at[k],
            device_id=device(to), device_id_type=MESH,
        )
        copy.start()
        started.append(copy)
        return copy

    def wait(copies):
        for copy in copies:
            copy.wait_recv()

    c = me["c"]
    recv0, acc, snd1, recv1, acc1, recv2, acc2, recv3 = (
        s[n] for n in ("recv0", "acc", "snd1", "recv1", "acc1", "recv2", "acc2", "recv3")
    )
    copies = [send(grads.at[pl.ds((1 - c) * N0, N0)], recv0, peer(me, "c", 1))]

    arrive(pg_up)
    arrive(pg_down)

    def edge(f):
        put(odd, f, 0, *rows_of(f, (0, 1)))
        put(odd, f, 4, *rows_of(f, (8, 9)))

    loop(4, edge)

    def cot_sum(n):
        f, r = n // 4, n % 4
        total = jnp.zeros((32, 256), F32)
        for q in range(4):
            total = total + cotp[f, pl.ds(r * 128 + q * 32, 32)].astype(F32)
        s["ig_acc"][pl.ds(n * 32, 32)] = total

    loop(16, cot_sum)

    wait(copies)

    def add0(i):
        at = pl.ds(i * 12, 12)
        total = grads[pl.ds(c * N0 + i * 12, 12)] + recv0[at]
        acc[at] = total
        snd1[at] = total.astype(BF16)

    loop(16, add0)
    order = (("x", "y"), ("y", "x"))
    copies = []
    for part in range(2):
        axis = order[part][0]
        for d in range(1, 4):
            to = peer(me, axis, d)
            copies.append(send(snd1.at[pl.ds(part * 96 + to[axis] * N1, N1)], recv1.at[part, d - 1], to))

    def inputs(j):
        total = nt(odd[j, :, 1:5].reshape(512, 256), wv[j])
        total = total + nt(even[j].reshape(512, 256), wv[3 + j])
        total = total + nt(odd[j, :, 0:4].reshape(512, 256), wv[6 + j])
        s["ig_acc"][...] += total

    loop(3, inputs)
    s["ig_v"][...] = s["ig_acc"][...].astype(BF16).reshape(4, 4, 32, 256)
    outs.append(local(s["ig_v"], ig_hbm))

    wait(copies)
    for part in range(2):
        mine = part * 96 + me[order[part][0]] * N1

        def add1(i, part=part, mine=mine):
            at = pl.ds(i * 6, 6)
            total = acc[pl.ds(mine + i * 6, 6)]
            for d in range(3):
                total = total + recv1[part, d, at].astype(F32)
            acc1[part, at] = total

        loop(4, add1)
    copies = []
    for part in range(2):
        axis = order[part][1]
        for d in range(1, 4):
            to = peer(me, axis, d)
            copies.append(send(acc1.at[part, pl.ds(to[axis] * N2, N2)], recv2.at[part, d - 1], to))
    wait(copies)
    for part in range(2):
        total = acc1[part, pl.ds(me[order[part][1]] * N2, N2)]
        for d in range(3):
            total = total + recv2[part, d]
        acc2[part] = total

    def zslice(z):
        return pl.ds((z % 4) // 2 * N3, N3), slice(None), pl.ds(pl.multiple_of((z % 2) * 128, 128), 128)

    copies = []
    for d in range(1, 8):
        to = peer(me, "z", d)
        copies.append(send(acc2.at[(to["z"] // 4, *zslice(to["z"]))], recv3.at[d - 1], to))
    wait(copies)
    z = me["z"]
    total = acc2[(z // 4, *zslice(z))]
    for d in range(7):
        total = total + recv3[d]
    part = z // 4
    first = (me["x"] * (1 - part) + me["y"] * part) * N1
    second = (me["y"] * (1 - part) + me["x"] * part) * N2
    base = c * N0 + part * 96 + first + second
    lanes = zslice(z)[2]
    shard = (pl.ds(base + (z % 4) // 2 * N3, N3), slice(None), lanes)
    full[shard] = total.astype(BF16)
    wait([send(full.at[shard], full.at[shard], peer(me, "z", d)) for d in range(1, 8)])
    copies = []
    for part in range(2):
        a, b = order[part]
        at = pl.ds(c * N0 + part * 96 + me[a] * N1 + me[b] * N2, N2)
        for d in range(1, 4):
            copies.append(send(full.at[at], full.at[at], peer(me, b, d)))
    wait(copies)
    copies = []
    for part in range(2):
        a, b = order[part]
        at = pl.ds(c * N0 + part * 96 + me[a] * N1, N1)
        for d in range(1, 4):
            copies.append(send(full.at[at], full.at[at], peer(me, a, d)))
    wait(copies)
    at = pl.ds(c * N0, N0)
    copies = [send(full.at[at], full.at[at], peer(me, "c", 1))]
    fin = s["fin"]

    def spread(first):
        def one(i):
            fin[pl.ds(first + i * 12, 12)] = full[pl.ds(first + i * 12, 12)].astype(F32)

        loop(16, one)

    spread(c * N0)
    wait(copies)
    spread((1 - c) * N0)
    outs.append(local(fin.at[pl.ds(0, 288)], s_hbm))
    outs.append(local(fin.at[pl.ds(288, 96)], tg_hbm))
    for copy in started:
        copy.wait_send()
    for copy, sends in halos:

        @pl.when(sends)
        def _(copy=copy):
            copy.wait_send()

    for copy in outs:
        copy.wait()


def on_device(low_frames, spatial_weight, temporal_weight, cotangent):
    any_space = pl.BlockSpec(memory_space=pl.ANY)
    outs = pl.pallas_call(
        kernel,
        out_shape=(
            jax.ShapeDtypeStruct((4, 8, 64, 256), BF16),
            jax.ShapeDtypeStruct((4, 4, 32, 256), BF16),
            jax.ShapeDtypeStruct((288, 8, 256), F32),
            jax.ShapeDtypeStruct((96, 8, 256), F32),
        ),
        in_specs=[any_space] * 4,
        out_specs=(any_space,) * 4,
        scratch_shapes=list(SCRATCH.values()),
        compiler_params=pltpu.CompilerParams(
            collective_id=0, has_side_effects=True, vmem_limit_bytes=60 << 20
        ),
        name="section",
    )(low_frames[0], spatial_weight.reshape(9, 256, 256), temporal_weight, cotangent[0])
    section_out, input_grad, spatial_grad, temporal_grad = outs
    return (
        section_out[None],
        input_grad[None],
        spatial_grad.reshape(3, 3, 256, 256),
        temporal_grad.reshape(3, 256, 256),
    )


def solution(mesh):
    in_specs = (P("dp", "tm", "height", None, None), P(), P(), P("dp", "tm", "height", None, None))
    out_specs = (P("dp", "tm", "height", None, None), P("dp", "tm", "height", None, None), P(), P())
    return jax.shard_map(
        on_device, mesh=mesh, in_specs=in_specs, out_specs=out_specs, check_vma=False
    )
```

time: 115 us -> 76 us (0.66)
  matrix products: 22.5 us -> 0 us
  Pallas kernels: 48.9 us -> 68.4 us
  starting transfers between devices: 19 us -> 0 us
  local copies, waits for them, and re-layouts: 16.6 us -> 6.68 us
  other arithmetic: 6.59 us -> 0 us
    dot_general x36 -> x0, matrix products: 22.5 us -> none  [the longest x9 5.58 us: on_device(): jnp.dot(piece, spatial_weight[i, j].T, preferred_element_type=jnp.float32)]
    pallas_call x1, Pallas kernels: 48.9 us -> 68.4 us  [on_device(): pl.pallas_call(kernel, out_shape=(jax.ShapeDtypeStruct((4, 8, 64, 256), B...]
    ppermute x6 -> x0, starting transfers between devices: 19 us -> none  [the longest x2 9.14 us: extended(): lax.ppermute(lax.slice_in_dim(block, block.shape[dim] - width, None, axis...]
    slice x8 -> x0, local copies, waits for them, and re-layouts: 8.37 us -> none  [the longest x2 4.54 us: spatial_apply(): piece = padded[:, i:i + rows, j:j + cols, :].reshape(-1, chan)]
    reshape x2 -> x0, local copies, waits for them, and re-layouts: 4.12 us -> none  [the longest x1 3.47 us: on_device(): total.reshape(frames, rows_low, 2, cols_low, 2, chan).sum(axis=(2, 4))]
    unnamed x12 -> x8, local copies, waits for them, and re-layouts: 2.67 us -> 6.68 us
    reduce_sum x1 -> x0, other arithmetic: 3.96 us -> none  [on_device(): total.reshape(frames, rows_low, 2, cols_low, 2, chan).sum(axis=(2, 4))]
    concatenate x5 -> x0, other arithmetic: 2.63 us -> none  [the longest x1 1.44 us: on_device(): grad_ext = jnp.concatenate([grad_out, later], 0)]
  transfers between devices with their start and end apart: 6 -> 0, of which waited for: 0 -> 0; matrix products, arithmetic and copies ran while one was open for 24% -> 0% of each run, Pallas kernels for 43% -> 0%
where the time goes in v2:
time: 76 us; the launch traced here: 75.8 us
  Pallas kernels  68.4 us (90%)
  local copies, waits for them, and re-layouts  6.68 us (9%)
    pallas_call x1, Pallas kernels, on_device(): pl.pallas_call(kernel, out_shape=(jax.ShapeDtypeStruct((4, 8, 64, 256), B...  68.4 us
    unnamed x8, local copies, waits for them, and re-layouts  6.68 us

profile of v2, /device:TPU:1, one launch (start us, length us, event | category | flops | bytes accessed | tf_op | source)
XLA Modules:
  0.0 75.8 jit_solution(6994409164959675899)
XLA Ops:
  0.6 68.4 %section.1 = (bf16[4,8,64,256]{3,2,1,0:T(8,128)(2,1)}, bf16[4,4,32,256]{3,2,1,0:T(8,128)(2,1)}, f32[288,8,256]{2,1,0:T(8,128)}, f32[96,8,256]{2,1,0:T(8,128)}) custom-call(bf16[4,4,32,256]{3,2,1,0:T(8,128)(2,1)} %bitcast.13, bf16[9,256,256]{2,1,0:T(8,128)(2,1)} %bitcast.8, bf16[3,256,256]{2,1,0:T(8,128)(2,1)} %t_hbm.1, bf16[4,8,64,256]{3,2,1,0:T(8,128)(2,1)} %bitcast.10), custom_call_target="tpu_custom_call" | custom-call | tf_op jit(solution)/shard_map/section/pallas_call | solution.py:462
  69.1 0.0 copy-start
  69.1 2.5 %copy.12 = bf16[1,4,8,64,256]{4,3,2,1,0:T(8,128)(2,1)} copy(bf16[1,4,8,64,256]{4,3,2,1,0:T(8,128)(2,1)} %bitcast.9) | data formatting | bytes 2097152
  71.5 1.7 %copy.13 = bf16[1,4,4,32,256]{4,3,2,1,0:T(8,128)(2,1)} copy(bf16[1,4,4,32,256]{4,3,2,1,0:T(8,128)(2,1)} %bitcast.12) | data formatting | bytes 524288
  73.2 0.0 copy-done
  73.2 0.0 copy-start.1
  73.2 1.4 %copy.14 = f32[3,3,256,256]{3,2,1,0:T(8,128)} copy(f32[3,3,256,256]{3,2,1,0:T(8,128)S(1)} %bitcast.7) | data formatting | bytes 4718592
  74.6 0.3 copy-done.1
  74.9 0.9 %copy.15 = f32[3,256,256]{2,1,0:T(8,128)} copy(f32[3,256,256]{2,1,0:T(8,128)S(1)} %bitcast.11) | data formatting | bytes 1572864
Async XLA Ops:
  69.1 4.1 %copy-start = (f32[288,8,256]{2,1,0:T(8,128)S(1)}, f32[288,8,256]{2,1,0:T(8,128)}, u32[]{:S(2)}) copy-start(f32[288,8,256]{2,1,0:T(8,128)} %get-tuple-element.10) | copy-start | bytes 7077892
  73.2 1.7 %copy-start.1 = (f32[96,8,256]{2,1,0:T(8,128)S(1)}, f32[96,8,256]{2,1,0:T(8,128)}, u32[]{:S(2)}) copy-start(f32[96,8,256]{2,1,0:T(8,128)} %get-tuple-element.11) | copy-start | bytes 2359300

commit v3 on v2

--- a/solution.py
+++ b/solution.py
@@ -8,7 +8,11 @@
 F32 = jnp.float32
 BF16 = jnp.bfloat16
 MESH = pl.DeviceIdType.MESH
-N0, N1, N2, N3 = 192, 24, 6, 3
+CHUNKS = 3
+N0, N1, N2, N3 = 64, 8, 2, 1
+HALF = N0 // 2
+PLACES = (9, 10, 11, 3, 0, 6, 1, 7, 4, 5, 2, 8)
+SLOT = [PLACES.index(m) for m in range(12)]
 SIZE = dict(x=4, y=4, z=8, c=2)
 
 
@@ -59,26 +63,23 @@
     odd=pltpu.VMEM((3, 4, 5, 32, 256), BF16),
     even=pltpu.VMEM((3, 4, 4, 32, 256), BF16),
     grads=pltpu.VMEM((384, 8, 256), F32),
-    so_v=pltpu.VMEM((4, 8, 64, 256), BF16),
     ig_acc=pltpu.VMEM((512, 256), F32),
-    ig_v=pltpu.VMEM((4, 4, 32, 256), BF16),
-    fin=pltpu.VMEM((384, 8, 256), F32),
-    recv0=pltpu.VMEM((N0, 8, 256), F32),
-    acc=pltpu.VMEM((N0, 8, 256), F32),
-    snd1=pltpu.VMEM((N0, 8, 256), BF16),
-    recv1=pltpu.VMEM((2, 3, N1, 8, 256), BF16),
-    acc1=pltpu.VMEM((2, N1, 8, 256), F32),
-    recv2=pltpu.VMEM((2, 3, N2, 8, 256), F32),
-    acc2=pltpu.VMEM((2, N2, 8, 256), F32),
-    recv3=pltpu.VMEM((7, N3, 8, 128), F32),
-    full=pltpu.VMEM((2 * N0, 8, 256), BF16),
-    ssem=pltpu.SemaphoreType.DMA((49,)),
-    rsem=pltpu.SemaphoreType.DMA((49,)),
+    recv0=pltpu.VMEM((CHUNKS, N0, 8, 256), F32),
+    acc=pltpu.VMEM((CHUNKS, N0, 8, 256), F32),
+    snd1=pltpu.VMEM((CHUNKS, N0, 8, 256), BF16),
+    recv1=pltpu.VMEM((CHUNKS, 2, 3, N1, 8, 256), BF16),
+    acc1=pltpu.VMEM((CHUNKS, 2, N1, 8, 256), F32),
+    recv2=pltpu.VMEM((CHUNKS, 2, 3, N2, 8, 256), F32),
+    acc2=pltpu.VMEM((CHUNKS, 2, N2, 8, 256), F32),
+    recv3=pltpu.VMEM((CHUNKS, 7, N3, 8, 128), F32),
+    full=pltpu.VMEM((CHUNKS * 2 * N0, 8, 256), BF16),
+    ssem=pltpu.SemaphoreType.DMA((9 + 40 * CHUNKS,)),
+    rsem=pltpu.SemaphoreType.DMA((9 + 40 * CHUNKS,)),
     lsem=pltpu.SemaphoreType.DMA((24,)),
 )
 
 
-def kernel(low_hbm, w_hbm, t_hbm, cot_hbm, so_hbm, ig_hbm, s_hbm, tg_hbm, *scratch):
+def kernel(low_hbm, w_hbm, t_hbm, cot_hbm, so_v, ig_v, s_v, tg_v, *scratch):
     s = dict(zip(SCRATCH, scratch))
     low, cot, cotp, ys, act, ds, pg = (s[n] for n in ("low", "cot", "cotp", "ys", "act", "ds", "pg"))
     odd, even, grads, tmp, full = (s[n] for n in ("odd", "even", "grads", "tmp", "full"))
@@ -241,7 +242,6 @@
         arrive(pair)
     products(0, 2)
     activate(0, 2, False)
-    outs = []
 
     def section(t):
         total = nn(act[t + 2], tv[0]) + nn(act[t + 1], tv[1]) + nn(act[t], tv[2])
@@ -254,10 +254,9 @@
                     tmp[y * 2 + half, pl.ds(b, 32, stride=2), :] = value[:, half * 128 : half * 128 + 128]
         for y in range(8):
             for half in range(2):
-                s["so_v"][t, y, :, half * 128 : half * 128 + 128] = tmp[y * 2 + half].astype(BF16)
+                so_v[t, y, :, half * 128 : half * 128 + 128] = tmp[y * 2 + half].astype(BF16)
 
     loop(4, section)
-    outs.append(local(s["so_v"], so_hbm))
 
     for f in range(2):
         arrive(cots[f])
@@ -270,7 +269,7 @@
         total = nn(s["actT"][0], cotp[k])
         for f in range(1, 4):
             total = total + nn(s["actT"][f], cotp[f + k])
-        grads[288 + 32 * k : 320 + 32 * k] = total.reshape(32, 8, 256)
+        grads[32 * k : 32 * k + 32] = total.reshape(32, 8, 256)
 
     def put(ref, f, q, even_cols, odd_cols):
         ref[0, f, q] = (odd_cols + from_right(even_cols)).astype(BF16)
@@ -294,14 +293,6 @@
             put(even, f, r, *rows_of(f, (2 * r + 1, 2 * r + 2)))
 
     loop(4, box)
-
-    def weight_grads(j):
-        sums = odd[j].reshape(640, 256)
-        grads[pl.ds(j * 32, 32)] = nn(s["lowT0"][...], sums).reshape(32, 8, 256)
-        grads[pl.ds((6 + j) * 32, 32)] = nn(s["lowT2"][...], sums).reshape(32, 8, 256)
-        grads[pl.ds((3 + j) * 32, 32)] = nn(s["lowT1"][...], even[j].reshape(512, 256)).reshape(32, 8, 256)
-
-    loop(3, weight_grads)
 
     started = []
 
@@ -316,24 +307,123 @@
         started.append(copy)
         return copy
 
-    def wait(copies):
-        for copy in copies:
-            copy.wait_recv()
-
-    c = me["c"]
+    def weight_grad(m):
+        i, j = m // 3, m % 3
+        if i == 1:
+            total = nn(s["lowT1"][...], even[j].reshape(512, 256))
+        else:
+            total = nn(s["lowT0" if i == 0 else "lowT2"][...], odd[j].reshape(640, 256))
+        at = SLOT[m] * 32
+        grads[at : at + 32] = total.reshape(32, 8, 256)
+
+    c, z = me["c"], me["z"]
+    order = (("x", "y"), ("y", "x"))
     recv0, acc, snd1, recv1, acc1, recv2, acc2, recv3 = (
         s[n] for n in ("recv0", "acc", "snd1", "recv1", "acc1", "recv2", "acc2", "recv3")
     )
-    copies = [send(grads.at[pl.ds((1 - c) * N0, N0)], recv0, peer(me, "c", 1))]
-
-    arrive(pg_up)
-    arrive(pg_down)
+
+    def base(k):
+        return k * 2 * N0 + c * N0
+
+    def zslice(to):
+        return pl.ds((to % 4) // 2, N3), slice(None), pl.ds(pl.multiple_of((to % 2) * 128, 128), 128)
+
+    def stage0(k):
+        for m in PLACES[4 * k : 4 * k + 4]:
+            if m < 9:
+                weight_grad(m)
+        return [send(grads.at[pl.ds(k * 2 * N0 + (1 - c) * N0, N0)], recv0.at[k], peer(me, "c", 1))]
+
+    def stage1(k):
+        def add(i):
+            at = pl.ds(i * 8, 8)
+            total = grads[pl.ds(base(k) + i * 8, 8)] + recv0[k, at]
+            acc[k, at] = total
+            snd1[k, at] = total.astype(BF16)
+
+        loop(N0 // 8, add)
+        copies = []
+        for part in range(2):
+            axis = order[part][0]
+            for d in range(1, 4):
+                to = peer(me, axis, d)
+                src = snd1.at[k, pl.ds(part * HALF + to[axis] * N1, N1)]
+                copies.append(send(src, recv1.at[k, part, d - 1], to))
+        return copies
+
+    def stage2(k):
+        for part in range(2):
+            total = acc[k, pl.ds(part * HALF + me[order[part][0]] * N1, N1)]
+            for d in range(3):
+                total = total + recv1[k, part, d].astype(F32)
+            acc1[k, part] = total
+        copies = []
+        for part in range(2):
+            axis = order[part][1]
+            for d in range(1, 4):
+                to = peer(me, axis, d)
+                copies.append(send(acc1.at[k, part, pl.ds(to[axis] * N2, N2)], recv2.at[k, part, d - 1], to))
+        return copies
+
+    def stage3(k):
+        for part in range(2):
+            total = acc1[k, part, pl.ds(me[order[part][1]] * N2, N2)]
+            for d in range(3):
+                total = total + recv2[k, part, d]
+            acc2[k, part] = total
+        copies = []
+        for d in range(1, 8):
+            to = peer(me, "z", d)
+            copies.append(send(acc2.at[(k, to["z"] // 4, *zslice(to["z"]))], recv3.at[k, d - 1], to))
+        return copies
+
+    def stage4(k):
+        total = acc2[(k, z // 4, *zslice(z))]
+        for d in range(7):
+            total = total + recv3[k, d]
+        part = z // 4
+        first = (me["x"] * (1 - part) + me["y"] * part) * N1
+        second = (me["y"] * (1 - part) + me["x"] * part) * N2
+        at = base(k) + part * HALF + first + second + (z % 4) // 2
+        shard = (pl.ds(at, N3), slice(None), zslice(z)[2])
+        full[shard] = total.astype(BF16)
+        return [send(full.at[shard], full.at[shard], peer(me, "z", d)) for d in range(1, 8)]
+
+    def spread_by(k, depth):
+        copies = []
+        for part in range(2):
+            a, b = order[part]
+            if depth == 2:
+                at, axis = pl.ds(base(k) + part * HALF + me[a] * N1 + me[b] * N2, N2), b
+            else:
+                at, axis = pl.ds(base(k) + part * HALF + me[a] * N1, N1), a
+            copies += [send(full.at[at], full.at[at], peer(me, axis, d)) for d in range(1, 4)]
+        return copies
+
+    def stage5(k):
+        return spread_by(k, 2)
+
+    def stage6(k):
+        return spread_by(k, 1)
+
+    def stage7(k):
+        at = pl.ds(base(k), N0)
+        return [send(full.at[at], full.at[at], peer(me, "c", 1))]
+
+    def stage8(k):
+        for n in range(4 * k, 4 * k + 4):
+            m = PLACES[n]
+            ref, at = (s_v, m) if m < 9 else (tg_v, m - 9)
+
+            def widen(i, n=n, ref=ref, at=at):
+                ref[pl.ds(at * 32 + i * 8, 8)] = full[pl.ds(n * 32 + i * 8, 8)].astype(F32)
+
+            loop(4, widen)
+        return []
 
     def edge(f):
         put(odd, f, 0, *rows_of(f, (0, 1)))
         put(odd, f, 4, *rows_of(f, (8, 9)))
-
-    loop(4, edge)
 
     def cot_sum(n):
         f, r = n // 4, n % 4
@@ -342,109 +432,29 @@
             total = total + cotp[f, pl.ds(r * 128 + q * 32, 32)].astype(F32)
         s["ig_acc"][pl.ds(n * 32, 32)] = total
 
-    loop(16, cot_sum)
-
-    wait(copies)
-
-    def add0(i):
-        at = pl.ds(i * 12, 12)
-        total = grads[pl.ds(c * N0 + i * 12, 12)] + recv0[at]
-        acc[at] = total
-        snd1[at] = total.astype(BF16)
-
-    loop(16, add0)
-    order = (("x", "y"), ("y", "x"))
-    copies = []
-    for part in range(2):
-        axis = order[part][0]
-        for d in range(1, 4):
-            to = peer(me, axis, d)
-            copies.append(send(snd1.at[pl.ds(part * 96 + to[axis] * N1, N1)], recv1.at[part, d - 1], to))
-
     def inputs(j):
         total = nt(odd[j, :, 1:5].reshape(512, 256), wv[j])
         total = total + nt(even[j].reshape(512, 256), wv[3 + j])
         total = total + nt(odd[j, :, 0:4].reshape(512, 256), wv[6 + j])
         s["ig_acc"][...] += total
 
-    loop(3, inputs)
-    s["ig_v"][...] = s["ig_acc"][...].astype(BF16).reshape(4, 4, 32, 256)
-    outs.append(local(s["ig_v"], ig_hbm))
-
-    wait(copies)
-    for part in range(2):
-        mine = part * 96 + me[order[part][0]] * N1
-
-        def add1(i, part=part, mine=mine):
-            at = pl.ds(i * 6, 6)
-            total = acc[pl.ds(mine + i * 6, 6)]
-            for d in range(3):
-                total = total + recv1[part, d, at].astype(F32)
-            acc1[part, at] = total
-
-        loop(4, add1)
-    copies = []
-    for part in range(2):
-        axis = order[part][1]
-        for d in range(1, 4):
-            to = peer(me, axis, d)
-            copies.append(send(acc1.at[part, pl.ds(to[axis] * N2, N2)], recv2.at[part, d - 1], to))
-    wait(copies)
-    for part in range(2):
-        total = acc1[part, pl.ds(me[order[part][1]] * N2, N2)]
-        for d in range(3):
-            total = total + recv2[part, d]
-        acc2[part] = total
-
-    def zslice(z):
-        return pl.ds((z % 4) // 2 * N3, N3), slice(None), pl.ds(pl.multiple_of((z % 2) * 128, 128), 128)
-
-    copies = []
-    for d in range(1, 8):
-        to = peer(me, "z", d)
-        copies.append(send(acc2.at[(to["z"] // 4, *zslice(to["z"]))], recv3.at[d - 1], to))
-    wait(copies)
-    z = me["z"]
-    total = acc2[(z // 4, *zslice(z))]
-    for d in range(7):
-        total = total + recv3[d]
-    part = z // 4
-    first = (me["x"] * (1 - part) + me["y"] * part) * N1
-    second = (me["y"] * (1 - part) + me["x"] * part) * N2
-    base = c * N0 + part * 96 + first + second
-    lanes = zslice(z)[2]
-    shard = (pl.ds(base + (z % 4) // 2 * N3, N3), slice(None), lanes)
-    full[shard] = total.astype(BF16)
-    wait([send(full.at[shard], full.at[shard], peer(me, "z", d)) for d in range(1, 8)])
-    copies = []
-    for part in range(2):
-        a, b = order[part]
-        at = pl.ds(c * N0 + part * 96 + me[a] * N1 + me[b] * N2, N2)
-        for d in range(1, 4):
-            copies.append(send(full.at[at], full.at[at], peer(me, b, d)))
-    wait(copies)
-    copies = []
-    for part in range(2):
-        a, b = order[part]
-        at = pl.ds(c * N0 + part * 96 + me[a] * N1, N1)
-        for d in range(1, 4):
-            copies.append(send(full.at[at], full.at[at], peer(me, a, d)))
-    wait(copies)
-    at = pl.ds(c * N0, N0)
-    copies = [send(full.at[at], full.at[at], peer(me, "c", 1))]
-    fin = s["fin"]
-
-    def spread(first):
-        def one(i):
-            fin[pl.ds(first + i * 12, 12)] = full[pl.ds(first + i * 12, 12)].astype(F32)
-
-        loop(16, one)
-
-    spread(c * N0)
-    wait(copies)
-    spread((1 - c) * N0)
-    outs.append(local(fin.at[pl.ds(0, 288)], s_hbm))
-    outs.append(local(fin.at[pl.ds(288, 96)], tg_hbm))
+    def input_grad():
+        arrive(pg_up)
+        arrive(pg_down)
+        loop(4, edge)
+        loop(16, cot_sum)
+        loop(3, inputs)
+        ig_v[...] = s["ig_acc"][...].astype(BF16).reshape(4, 4, 32, 256)
+
+    stages = (stage0, stage1, stage2, stage3, stage4, stage5, stage6, stage7, stage8)
+    flying = [[] for _ in range(CHUNKS)]
+    for stage in stages:
+        for k in range(CHUNKS):
+            for copy in flying[k]:
+                copy.wait_recv()
+            flying[k] = stage(k)
+        if stage is stage1:
+            input_grad()
     for copy in started:
         copy.wait_send()
     for copy, sends in halos:
@@ -453,28 +463,47 @@
         def _(copy=copy):
             copy.wait_send()
 
-    for copy in outs:
+
+def store(so_v, ig_v, s_v, tg_v, so, ig, sg, tg, sems):
+    copies = [
+        pltpu.make_async_copy(src, dst, sems.at[n])
+        for n, (src, dst) in enumerate(((so_v, so), (s_v, sg), (tg_v, tg), (ig_v, ig)))
+    ]
+    for copy in copies:
+        copy.start()
+    for copy in copies:
         copy.wait()
 
 
 def on_device(low_frames, spatial_weight, temporal_weight, cotangent):
-    any_space = pl.BlockSpec(memory_space=pl.ANY)
-    outs = pl.pallas_call(
+    hbm = pl.BlockSpec(memory_space=pltpu.HBM)
+    vmem = pl.BlockSpec(memory_space=pltpu.VMEM)
+    shapes = (
+        jax.ShapeDtypeStruct((4, 8, 64, 256), BF16),
+        jax.ShapeDtypeStruct((4, 4, 32, 256), BF16),
+        jax.ShapeDtypeStruct((288, 8, 256), F32),
+        jax.ShapeDtypeStruct((96, 8, 256), F32),
+    )
+    held = pl.pallas_call(
         kernel,
-        out_shape=(
-            jax.ShapeDtypeStruct((4, 8, 64, 256), BF16),
-            jax.ShapeDtypeStruct((4, 4, 32, 256), BF16),
-            jax.ShapeDtypeStruct((288, 8, 256), F32),
-            jax.ShapeDtypeStruct((96, 8, 256), F32),
-        ),
-        in_specs=[any_space] * 4,
-        out_specs=(any_space,) * 4,
+        out_shape=tuple(pltpu.VMEM(a.shape, a.dtype) for a in shapes),
+        in_specs=[hbm] * 4,
+        out_specs=(vmem,) * 4,
         scratch_shapes=list(SCRATCH.values()),
         compiler_params=pltpu.CompilerParams(
-            collective_id=0, has_side_effects=True, vmem_limit_bytes=60 << 20
+            collective_id=0, has_side_effects=True, vmem_limit_bytes=52 << 20
         ),
         name="section",
     )(low_frames[0], spatial_weight.reshape(9, 256, 256), temporal_weight, cotangent[0])
+    outs = pl.pallas_call(
+        store,
+        out_shape=shapes,
+        in_specs=[vmem] * 4,
+        out_specs=(hbm,) * 4,
+        scratch_shapes=[pltpu.SemaphoreType.DMA((4,))],
+        compiler_params=pltpu.CompilerParams(vmem_limit_bytes=4 << 20),
+        name="store",
+    )(*(pltpu.with_memory_space_constraint(a, pltpu.VMEM) for a in held))
     section_out, input_grad, spatial_grad, temporal_grad = outs
     return (
         section_out[None],

time: 76 us -> 64.5 us (0.85)
  local copies, waits for them, and re-layouts: 6.68 us -> 0 us
  Pallas kernels: 68.4 us -> 63.7 us
    unnamed x8 -> x0, local copies, waits for them, and re-layouts: 6.68 us -> none
    pallas_call x1 -> x2, Pallas kernels: 68.4 us -> 63.7 us  [the longest x1 61.6 us: on_device(): pl.pallas_call(kernel, out_shape=tuple((pltpu.VMEM(a.shape, a.dtype) for...]
where the time goes in v3:
time: 64.5 us; the launch traced here: 64.4 us
  Pallas kernels  63.7 us (99%)
    pallas_call x1, Pallas kernels, on_device(): pl.pallas_call(kernel, out_shape=tuple((pltpu.VMEM(a.shape, a.dtype) for...  61.6 us
    pallas_call x1, Pallas kernels, on_device(): pl.pallas_call(store, out_shape=shapes, in_specs=[vmem] * 4, out_specs=(h...  2.12 us

profile of v3, /device:TPU:1, one launch (start us, length us, event | category | flops | bytes accessed | tf_op | source)
XLA Modules:
  0.0 64.4 jit_solution(6601895194210078211)
XLA Ops:
  0.6 61.6 %section.1 = (bf16[4,8,64,256]{3,2,1,0:T(8,128)(2,1)S(1)}, bf16[4,4,32,256]{3,2,1,0:T(8,128)(2,1)S(1)}, f32[288,8,256]{2,1,0:T(8,128)S(1)}, f32[96,8,256]{2,1,0:T(8,128)S(1)}) custom-call(bf16[4,4,32,256]{3,2,1,0:T(8,128)(2,1)} %bitcast.9, bf16[9,256,256]{2,1,0:T(8,128)(2,1)} %bitcast.7, bf16[3,256,256]{2,1,0:T(8,128)(2,1)} %t_hbm.1, ...), custom_call_target="tpu_custom_call" | custom-call | tf_op jit(solution)/shard_map/section/pallas_call | solution.py:487
  62.3 2.1 %store.1 = (bf16[4,8,64,256]{3,2,1,0:T(8,128)(2,1)}, bf16[4,4,32,256]{3,2,1,0:T(8,128)(2,1)}, f32[288,8,256]{2,1,0:T(8,128)}, f32[96,8,256]{2,1,0:T(8,128)}) custom-call(bf16[4,8,64,256]{3,2,1,0:T(8,128)(2,1)S(1)} %get-tuple-element.12.so_v, bf16[4,4,32,256]{3,2,1,0:T(8,128)(2,1)S(1)} %get-tuple-element.13.ig_v, f32[288,8,256]{2,1,0:T(8,128)S(1)} %get-tuple-element.14.s_v, ...), custom_call_target="tpu_custom_call" | custom-call | tf_op jit(solution)/shard_map/store/pallas_call | solution.py:498

commit v4 on v3

--- a/solution.py
+++ b/solution.py
@@ -54,27 +54,28 @@
     tmp=pltpu.VMEM((16, 64, 128), F32),
     ys=pltpu.VMEM((9, 24, 32, 256), F32),
     act=pltpu.VMEM((6, 512, 256), BF16),
-    actT=pltpu.VMEM((4, 256, 512), BF16),
-    lowT0=pltpu.VMEM((256, 640), BF16),
-    lowT1=pltpu.VMEM((256, 512), BF16),
-    lowT2=pltpu.VMEM((256, 640), BF16),
+    actT=pltpu.VMEM((256, 2048), BF16),
+    lowT=pltpu.VMEM((2, 256, 384), BF16),
+    tT=pltpu.VMEM((768, 256), BF16),
     ds=pltpu.VMEM((4, 512, 256), F32),
     pg=pltpu.VMEM((4, 10, 64, 256), BF16),
-    odd=pltpu.VMEM((3, 4, 5, 32, 256), BF16),
-    even=pltpu.VMEM((3, 4, 4, 32, 256), BF16),
+    odd=pltpu.VMEM((3, 4, 7, 32, 256), BF16),
+    even=pltpu.VMEM((3, 4, 6, 32, 256), BF16),
     grads=pltpu.VMEM((384, 8, 256), F32),
     ig_acc=pltpu.VMEM((512, 256), F32),
     recv0=pltpu.VMEM((CHUNKS, N0, 8, 256), F32),
     acc=pltpu.VMEM((CHUNKS, N0, 8, 256), F32),
-    snd1=pltpu.VMEM((CHUNKS, N0, 8, 256), BF16),
-    recv1=pltpu.VMEM((CHUNKS, 2, 3, N1, 8, 256), BF16),
+    snd1=pltpu.VMEM((CHUNKS, N0 // 2, 16, 256), BF16),
+    recv1=pltpu.VMEM((CHUNKS, 2, 3, N1 // 2, 16, 256), BF16),
     acc1=pltpu.VMEM((CHUNKS, 2, N1, 8, 256), F32),
     recv2=pltpu.VMEM((CHUNKS, 2, 3, N2, 8, 256), F32),
     acc2=pltpu.VMEM((CHUNKS, 2, N2, 8, 256), F32),
     recv3=pltpu.VMEM((CHUNKS, 7, N3, 8, 128), F32),
-    full=pltpu.VMEM((CHUNKS * 2 * N0, 8, 256), BF16),
+    mean=pltpu.VMEM((CHUNKS, 2, N2, 8, 256), F32),
+    full=pltpu.VMEM((CHUNKS * N0, 16, 256), BF16),
     ssem=pltpu.SemaphoreType.DMA((9 + 40 * CHUNKS,)),
     rsem=pltpu.SemaphoreType.DMA((9 + 40 * CHUNKS,)),
+    ready=pltpu.SemaphoreType.REGULAR((5,)),
     lsem=pltpu.SemaphoreType.DMA((24,)),
 )
 
@@ -88,7 +89,8 @@
     dp, tm, h = lax.axis_index("dp"), lax.axis_index("tm"), lax.axis_index("height")
     yes = True
     barrier = pltpu.get_barrier_semaphore()
-    others = [device(peer(me, axis, d)) for axis in ("c", "x", "y", "z") for d in range(1, SIZE[axis])]
+    near = [device(peer(me, axis, d)) for axis in "xyz" for d in (1, SIZE[axis] - 1)]
+    others = [device(peer(me, "c", 1))] + near
     others += [(dp, (tm + i) % 4, (h + j) % 8) for i in (0, 1, 3) for j in (1, 7)]
     for to in others:
         pl.semaphore_signal(barrier, inc=1, device_id=to, device_id_type=MESH)
@@ -172,22 +174,32 @@
         halo(low_hbm.at[last, 0], low.at[early, 5], (dp, right, down), (tm < 3) & (h > 0), (tm > 0) & (h < 7)),
     ]
 
+    def tell(slot, axis):
+        for d in (1, SIZE[axis] - 1):
+            to = device(peer(me, axis, d))
+            pl.semaphore_signal(s["ready"].at[slot], inc=1, device_id=to, device_id_type=MESH)
+
+    for slot, axis in enumerate("xyz"):
+        tell(slot, axis)
+
     def split_columns(f):
-        def row(y):
+        for y in range(8):
             for half in range(2):
-                lanes = pl.ds(half * 128, 128)
-                tmp[y * 2 + half] = cot[f, y, :, lanes].astype(F32)
+                tmp[y * 2 + half] = cot[f, y, :, half * 128 : half * 128 + 128].astype(F32)
+        for y in range(8):
+            for half in range(2):
                 for b in range(2):
                     part = tmp[y * 2 + half, pl.ds(b, 32, stride=2), :]
-                    cotp[f, pl.ds(y * 64 + b * 32, 32), lanes] = part.astype(BF16)
-
-        loop(8, row)
+                    at = pl.ds(y * 64 + b * 32, 32)
+                    cotp[f, at, half * 128 : half * 128 + 128] = part.astype(BF16)
 
     load_cot.wait()
     loop(4, split_columns)
     load_low.wait()
     load_w.wait()
     load_t.wait()
+    for k in range(3):
+        s["tT"][256 * k : 256 * k + 256] = tv[k].T
     arrive(low_up)
     arrive(low_down)
     col = lax.broadcasted_iota(jnp.int32, (32, 256), 0)
@@ -214,7 +226,7 @@
                 pres = (from_left(z[0]) + z[1] + z[2], z[0] + z[1] + from_right(z[2]))
                 for b in range(2):
                     pre = pres[b]
-                    sig = jax.nn.sigmoid(pre)
+                    sig = 0.5 * jnp.tanh(0.5 * pre) + 0.5
                     tokens = pl.ds((r * 2 + a) * 64 + b * 32, 32)
                     act[first + f, tokens] = (pre * sig).astype(BF16)
                     if slopes:
@@ -223,28 +235,95 @@
         loop(count * 4, one)
 
     products(2, 4)
+    for slot in range(3):
+        pl.semaphore_wait(s["ready"].at[slot], 2)
+    tell(3, "z")
     activate(2, 4, True)
-
-    def flip(f):
-        s["actT"][f] = act[2 + f].T
-
-    loop(4, flip)
-    s["lowT0"][...] = low[2:6, 0:5].reshape(640, 256).T
-    s["lowT1"][...] = low[2:6, 1:5].reshape(512, 256).T
-    s["lowT2"][...] = low[2:6, 1:6].reshape(640, 256).T
+    pl.semaphore_wait(s["ready"].at[3], 2)
+    tell(4, "z")
+
+    for f in range(4):
+        s["actT"][:, 512 * f : 512 * f + 512] = act[2 + f].T
+    for half in range(2):
+        s["lowT"][half] = low[2 + 2 * half : 4 + 2 * half].reshape(384, 256).T
+    pad = jnp.zeros((3, 4, 32, 256), BF16)
+    odd[:, :, 0] = pad
+    odd[:, :, 6] = pad
+    even[:, :, 0] = pad
+    even[:, :, 5] = pad
 
     def pre_grad(f):
-        total = nt(cotp[f], tv[0]) + nt(cotp[f + 1], tv[1]) + nt(cotp[f + 2], tv[2])
+        total = nn(jnp.concatenate([cotp[f + k] for k in range(3)], 1), s["tT"][...])
         pg[f, 1:9] = (total * ds[f]).astype(BF16).reshape(8, 64, 256)
 
+    def put(ref, f, q, even_cols, odd_cols):
+        ref[0, f, q + 1] = (odd_cols + from_right(even_cols)).astype(BF16)
+        ref[1, f, q + 1] = (odd_cols + even_cols).astype(BF16)
+        ref[2, f, q + 1] = (from_left(odd_cols) + even_cols).astype(BF16)
+
+    def rows_of(f, slots):
+        halves = []
+        for b in range(2):
+            total = pg[f, slots[0], b * 32 : b * 32 + 32].astype(F32)
+            for slot in slots[1:]:
+                total = total + pg[f, slot, b * 32 : b * 32 + 32].astype(F32)
+            halves.append(total)
+        return halves
+
+    def box(f):
+        for q in range(5):
+            slots = [n for n in (2 * q, 2 * q + 1) if 0 < n < 9]
+            put(odd, f, q, *rows_of(f, slots))
+        for r in range(4):
+            put(even, f, r, *rows_of(f, (2 * r + 1, 2 * r + 2)))
+
+    def weight_grad(m, half):
+        i, j = m // 3, m % 3
+        two = pl.ds(2 * half, 2)
+        sums = (odd[j, two, 1:7], even[j, two], odd[j, two, 0:6])[i]
+        total = nn(s["lowT"][half], sums.reshape(384, 256))
+        add_to(m, total, half == 0)
+
+    def add_to(m, total, fresh):
+        at = pl.ds(SLOT[m] * 32, 32)
+        total = total.reshape(32, 8, 256)
+        grads[at] = total if fresh else grads[at] + total
+
+    def temporal(k, frames, fresh):
+        a, b = frames[0], frames[-1] + 1
+        grad = cotp[a + k : b + k].reshape((b - a) * 512, 256)
+        total = nn(s["actT"][:, 512 * a : 512 * b], grad)
+        add_to(9 + k, total, fresh)
+
     loop(2, pre_grad)
-    for pair in early_low:
-        arrive(pair)
-    products(0, 2)
-    activate(0, 2, False)
+    pl.semaphore_wait(s["ready"].at[4], 2)
+    loop(2, box)
+    for k in range(3):
+        temporal(k, range(4 - k), True)
+    for m in range(9):
+        weight_grad(m, 0)
+    arrive(cots[0])
+    split_columns(4)
+    pre_grad(2)
+    temporal(1, (3,), False)
+    temporal(2, (2,), False)
+    box(2)
+    arrive(cots[1])
+    split_columns(5)
+    pre_grad(3)
+    pg_up = halo(pg.at[:, 8], pg.at[:, 0], (dp, tm, up), h < 7, h > 0)
+    pg_down = halo(pg.at[:, 1], pg.at[:, 9], (dp, tm, down), h > 0, h < 7)
+    temporal(2, (3,), False)
+    box(3)
+
+    def early():
+        for pair in early_low:
+            arrive(pair)
+        products(0, 2)
+        activate(0, 2, False)
 
     def section(t):
-        total = nn(act[t + 2], tv[0]) + nn(act[t + 1], tv[1]) + nn(act[t], tv[2])
+        total = nn(jnp.concatenate([act[t + 2 - k] for k in range(3)], 1), tv[...].reshape(768, 256))
         for y in range(8):
             up_row = low[t + 2, y // 2 + 1].astype(F32)
             for b in range(2):
@@ -256,44 +335,6 @@
             for half in range(2):
                 so_v[t, y, :, half * 128 : half * 128 + 128] = tmp[y * 2 + half].astype(BF16)
 
-    loop(4, section)
-
-    for f in range(2):
-        arrive(cots[f])
-        split_columns(4 + f)
-        pre_grad(2 + f)
-    pg_up = halo(pg.at[:, 8], pg.at[:, 0], (dp, tm, up), h < 7, h > 0)
-    pg_down = halo(pg.at[:, 1], pg.at[:, 9], (dp, tm, down), h > 0, h < 7)
-
-    for k in range(3):
-        total = nn(s["actT"][0], cotp[k])
-        for f in range(1, 4):
-            total = total + nn(s["actT"][f], cotp[f + k])
-        grads[32 * k : 32 * k + 32] = total.reshape(32, 8, 256)
-
-    def put(ref, f, q, even_cols, odd_cols):
-        ref[0, f, q] = (odd_cols + from_right(even_cols)).astype(BF16)
-        ref[1, f, q] = (odd_cols + even_cols).astype(BF16)
-        ref[2, f, q] = (from_left(odd_cols) + even_cols).astype(BF16)
-
-    def rows_of(f, slots):
-        halves = []
-        for b in range(2):
-            total = pg[f, slots[0], b * 32 : b * 32 + 32].astype(F32)
-            for slot in slots[1:]:
-                total = total + pg[f, slot, b * 32 : b * 32 + 32].astype(F32)
-            halves.append(total)
-        return halves
-
-    def box(f):
-        for q in range(5):
-            slots = [n for n in (2 * q, 2 * q + 1) if 0 < n < 9]
-            put(odd, f, q, *rows_of(f, slots))
-        for r in range(4):
-            put(even, f, r, *rows_of(f, (2 * r + 1, 2 * r + 2)))
-
-    loop(4, box)
-
     started = []
 
     def send(src, dst, to):
@@ -307,15 +348,6 @@
         started.append(copy)
         return copy
 
-    def weight_grad(m):
-        i, j = m // 3, m % 3
-        if i == 1:
-            total = nn(s["lowT1"][...], even[j].reshape(512, 256))
-        else:
-            total = nn(s["lowT0" if i == 0 else "lowT2"][...], odd[j].reshape(640, 256))
-        at = SLOT[m] * 32
-        grads[at : at + 32] = total.reshape(32, 8, 256)
-
     c, z = me["c"], me["z"]
     order = (("x", "y"), ("y", "x"))
     recv0, acc, snd1, recv1, acc1, recv2, acc2, recv3 = (
@@ -331,7 +363,7 @@
     def stage0(k):
         for m in PLACES[4 * k : 4 * k + 4]:
             if m < 9:
-                weight_grad(m)
+                weight_grad(m, 1)
         return [send(grads.at[pl.ds(k * 2 * N0 + (1 - c) * N0, N0)], recv0.at[k], peer(me, "c", 1))]
 
     def stage1(k):
@@ -339,7 +371,7 @@
             at = pl.ds(i * 8, 8)
             total = grads[pl.ds(base(k) + i * 8, 8)] + recv0[k, at]
             acc[k, at] = total
-            snd1[k, at] = total.astype(BF16)
+            snd1[k, pl.ds(i * 4, 4)] = total.reshape(4, 16, 256).astype(BF16)
 
         loop(N0 // 8, add)
         copies = []
@@ -347,7 +379,7 @@
             axis = order[part][0]
             for d in range(1, 4):
                 to = peer(me, axis, d)
-                src = snd1.at[k, pl.ds(part * HALF + to[axis] * N1, N1)]
+                src = snd1.at[k, pl.ds((part * HALF + to[axis] * N1) // 2, N1 // 2)]
                 copies.append(send(src, recv1.at[k, part, d - 1], to))
         return copies
 
@@ -355,7 +387,7 @@
         for part in range(2):
             total = acc[k, pl.ds(part * HALF + me[order[part][0]] * N1, N1)]
             for d in range(3):
-                total = total + recv1[k, part, d].astype(F32)
+                total = total + recv1[k, part, d].astype(F32).reshape(N1, 8, 256)
             acc1[k, part] = total
         copies = []
         for part in range(2):
@@ -381,22 +413,23 @@
         total = acc2[(k, z // 4, *zslice(z))]
         for d in range(7):
             total = total + recv3[k, d]
-        part = z // 4
-        first = (me["x"] * (1 - part) + me["y"] * part) * N1
-        second = (me["y"] * (1 - part) + me["x"] * part) * N2
-        at = base(k) + part * HALF + first + second + (z % 4) // 2
-        shard = (pl.ds(at, N3), slice(None), zslice(z)[2])
-        full[shard] = total.astype(BF16)
-        return [send(full.at[shard], full.at[shard], peer(me, "z", d)) for d in range(1, 8)]
+        shard = s["mean"].at[(k, z // 4, *zslice(z))]
+        shard[...] = total
+        return [send(shard, shard, peer(me, "z", d)) for d in range(1, 8)]
+
+    def unit(k, n):
+        return k * N0 + (c * N0 + n) // 2
 
     def spread_by(k, depth):
         copies = []
         for part in range(2):
             a, b = order[part]
             if depth == 2:
-                at, axis = pl.ds(base(k) + part * HALF + me[a] * N1 + me[b] * N2, N2), b
+                n = unit(k, part * HALF + me[a] * N1 + me[b] * N2)
+                full[n] = s["mean"][k, part].reshape(16, 256).astype(BF16)
+                at, axis = pl.ds(n, N2 // 2), b
             else:
-                at, axis = pl.ds(base(k) + part * HALF + me[a] * N1, N1), a
+                at, axis = pl.ds(unit(k, part * HALF + me[a] * N1), N1 // 2), a
             copies += [send(full.at[at], full.at[at], peer(me, axis, d)) for d in range(1, 4)]
         return copies
 
@@ -407,7 +440,7 @@
         return spread_by(k, 1)
 
     def stage7(k):
-        at = pl.ds(base(k), N0)
+        at = pl.ds(unit(k, 0), N0 // 2)
         return [send(full.at[at], full.at[at], peer(me, "c", 1))]
 
     def stage8(k):
@@ -416,7 +449,7 @@
             ref, at = (s_v, m) if m < 9 else (tg_v, m - 9)
 
             def widen(i, n=n, ref=ref, at=at):
-                ref[pl.ds(at * 32 + i * 8, 8)] = full[pl.ds(n * 32 + i * 8, 8)].astype(F32)
+                ref[pl.ds(at * 32 + i * 8, 8)] = full[pl.ds(n * 16 + i * 4, 4)].astype(F32).reshape(8, 8, 256)
 
             loop(4, widen)
         return []
@@ -433,9 +466,9 @@
         s["ig_acc"][pl.ds(n * 32, 32)] = total
 
     def inputs(j):
-        total = nt(odd[j, :, 1:5].reshape(512, 256), wv[j])
-        total = total + nt(even[j].reshape(512, 256), wv[3 + j])
-        total = total + nt(odd[j, :, 0:4].reshape(512, 256), wv[6 + j])
+        total = nt(odd[j, :, 2:6].reshape(512, 256), wv[j])
+        total = total + nt(even[j, :, 1:5].reshape(512, 256), wv[3 + j])
+        total = total + nt(odd[j, :, 1:5].reshape(512, 256), wv[6 + j])
         s["ig_acc"][...] += total
 
     def input_grad():
@@ -455,6 +488,12 @@
             flying[k] = stage(k)
         if stage is stage1:
             input_grad()
+        if stage is stage2:
+            early()
+        if stage is stage3:
+            loop(2, section)
+        if stage is stage4:
+            loop(2, lambda t: section(t + 2))
     for copy in started:
         copy.wait_send()
     for copy, sends in halos:

time: 64.5 us -> 60.6 us (0.940)
  Pallas kernels: 63.7 us -> 59.9 us
    pallas_call x1, Pallas kernels: 61.6 us -> 57.8 us  [on_device(): pl.pallas_call(kernel, out_shape=tuple((pltpu.VMEM(a.shape, a.dtype) for...]
where the time goes in v4:
time: 60.6 us; the launch traced here: 60.5 us
  Pallas kernels  59.9 us (99%)
  between operations  0.64 us (1%)
    pallas_call x1, Pallas kernels, on_device(): pl.pallas_call(kernel, out_shape=tuple((pltpu.VMEM(a.shape, a.dtype) for...  57.8 us
    pallas_call x1, Pallas kernels, on_device(): pl.pallas_call(store, out_shape=shapes, in_specs=[vmem] * 4, out_specs=(h...  2.12 us

profile of v4, /device:TPU:1, one launch (start us, length us, event | category | flops | bytes accessed | tf_op | source)
XLA Modules:
  0.0 60.5 jit_solution(7789628200125629432)
XLA Ops:
  0.6 57.8 %section.1 = (bf16[4,8,64,256]{3,2,1,0:T(8,128)(2,1)S(1)}, bf16[4,4,32,256]{3,2,1,0:T(8,128)(2,1)S(1)}, f32[288,8,256]{2,1,0:T(8,128)S(1)}, f32[96,8,256]{2,1,0:T(8,128)S(1)}) custom-call(bf16[4,4,32,256]{3,2,1,0:T(8,128)(2,1)} %bitcast.9, bf16[9,256,256]{2,1,0:T(8,128)(2,1)} %bitcast.7, bf16[3,256,256]{2,1,0:T(8,128)(2,1)} %t_hbm.1, ...), custom_call_target="tpu_custom_call" | custom-call | tf_op jit(solution)/shard_map/section/pallas_call | solution.py:526
  58.4 2.1 %store.1 = (bf16[4,8,64,256]{3,2,1,0:T(8,128)(2,1)}, bf16[4,4,32,256]{3,2,1,0:T(8,128)(2,1)}, f32[288,8,256]{2,1,0:T(8,128)}, f32[96,8,256]{2,1,0:T(8,128)}) custom-call(bf16[4,8,64,256]{3,2,1,0:T(8,128)(2,1)S(1)} %get-tuple-element.12.so_v, bf16[4,4,32,256]{3,2,1,0:T(8,128)(2,1)S(1)} %get-tuple-element.13.ig_v, f32[288,8,256]{2,1,0:T(8,128)S(1)} %get-tuple-element.14.s_v, ...), custom_call_target="tpu_custom_call" | custom-call | tf_op jit(solution)/shard_map/store/pallas_call | solution.py:537

commit v5 on v4

--- a/solution.py
+++ b/solution.py
@@ -11,6 +11,7 @@
 CHUNKS = 3
 N0, N1, N2, N3 = 64, 8, 2, 1
 HALF = N0 // 2
+FAR_FIRST = (4, 3, 5, 2, 6, 1, 7)
 PLACES = (9, 10, 11, 3, 0, 6, 1, 7, 4, 5, 2, 8)
 SLOT = [PLACES.index(m) for m in range(12)]
 SIZE = dict(x=4, y=4, z=8, c=2)
@@ -335,8 +336,6 @@
             for half in range(2):
                 so_v[t, y, :, half * 128 : half * 128 + 128] = tmp[y * 2 + half].astype(BF16)
 
-    started = []
-
     def send(src, dst, to):
         k = used[0]
         used[0] += 1
@@ -345,7 +344,6 @@
             device_id=device(to), device_id_type=MESH,
         )
         copy.start()
-        started.append(copy)
         return copy
 
     c, z = me["c"], me["z"]
@@ -377,7 +375,7 @@
         copies = []
         for part in range(2):
             axis = order[part][0]
-            for d in range(1, 4):
+            for d in (2, 1, 3):
                 to = peer(me, axis, d)
                 src = snd1.at[k, pl.ds((part * HALF + to[axis] * N1) // 2, N1 // 2)]
                 copies.append(send(src, recv1.at[k, part, d - 1], to))
@@ -392,7 +390,7 @@
         copies = []
         for part in range(2):
             axis = order[part][1]
-            for d in range(1, 4):
+            for d in (2, 1, 3):
                 to = peer(me, axis, d)
                 copies.append(send(acc1.at[k, part, pl.ds(to[axis] * N2, N2)], recv2.at[k, part, d - 1], to))
         return copies
@@ -404,7 +402,7 @@
                 total = total + recv2[k, part, d]
             acc2[k, part] = total
         copies = []
-        for d in range(1, 8):
+        for d in FAR_FIRST:
             to = peer(me, "z", d)
             copies.append(send(acc2.at[(k, to["z"] // 4, *zslice(to["z"]))], recv3.at[k, d - 1], to))
         return copies
@@ -415,7 +413,7 @@
             total = total + recv3[k, d]
         shard = s["mean"].at[(k, z // 4, *zslice(z))]
         shard[...] = total
-        return [send(shard, shard, peer(me, "z", d)) for d in range(1, 8)]
+        return [send(shard, shard, peer(me, "z", d)) for d in FAR_FIRST]
 
     def unit(k, n):
         return k * N0 + (c * N0 + n) // 2
@@ -430,7 +428,7 @@
                 at, axis = pl.ds(n, N2 // 2), b
             else:
                 at, axis = pl.ds(unit(k, part * HALF + me[a] * N1), N1 // 2), a
-            copies += [send(full.at[at], full.at[at], peer(me, axis, d)) for d in range(1, 4)]
+            copies += [send(full.at[at], full.at[at], peer(me, axis, d)) for d in (2, 1, 3)]
         return copies
 
     def stage5(k):
@@ -485,29 +483,31 @@
         for k in range(CHUNKS):
             for copy in flying[k]:
                 copy.wait_recv()
+            before = flying[k]
             flying[k] = stage(k)
+            for copy in before:
+                copy.wait_send()
         if stage is stage1:
             input_grad()
+            for copy, sends in halos:
+
+                @pl.when(sends)
+                def _(copy=copy):
+                    copy.wait_send()
+
         if stage is stage2:
             early()
         if stage is stage3:
             loop(2, section)
         if stage is stage4:
             loop(2, lambda t: section(t + 2))
-    for copy in started:
-        copy.wait_send()
-    for copy, sends in halos:
-
-        @pl.when(sends)
-        def _(copy=copy):
-            copy.wait_send()
-
 
 def store(so_v, ig_v, s_v, tg_v, so, ig, sg, tg, sems):
-    copies = [
-        pltpu.make_async_copy(src, dst, sems.at[n])
-        for n, (src, dst) in enumerate(((so_v, so), (s_v, sg), (tg_v, tg), (ig_v, ig)))
-    ]
+    pairs = [(s_v.at[pl.ds(n * 32, 32)], sg.at[pl.ds(n * 32, 32)]) for n in range(9)]
+    pairs += [(so_v.at[n], so.at[n]) for n in range(4)]
+    pairs += [(tg_v.at[pl.ds(n * 32, 32)], tg.at[pl.ds(n * 32, 32)]) for n in range(3)]
+    pairs.append((ig_v, ig))
+    copies = [pltpu.make_async_copy(src, dst, sems.at[n]) for n, (src, dst) in enumerate(pairs)]
     for copy in copies:
         copy.start()
     for copy in copies:
@@ -539,7 +539,7 @@
         out_shape=shapes,
         in_specs=[vmem] * 4,
         out_specs=(hbm,) * 4,
-        scratch_shapes=[pltpu.SemaphoreType.DMA((4,))],
+        scratch_shapes=[pltpu.SemaphoreType.DMA((17,))],
         compiler_params=pltpu.CompilerParams(vmem_limit_bytes=4 << 20),
         name="store",
     )(*(pltpu.with_memory_space_constraint(a, pltpu.VMEM) for a in held))

time: 60.6 us -> 59.6 us (0.983)
  Pallas kernels: 59.9 us -> 58.9 us
    pallas_call x1, Pallas kernels: 57.8 us -> 56.7 us  [on_device(): pl.pallas_call(kernel, out_shape=tuple((pltpu.VMEM(a.shape, a.dtype) for...]
where the time goes in v5:
time: 59.6 us; the launch traced here: 59.5 us
  Pallas kernels  58.9 us (99%)
  between operations  0.64 us (1%)
    pallas_call x1, Pallas kernels, on_device(): pl.pallas_call(kernel, out_shape=tuple((pltpu.VMEM(a.shape, a.dtype) for...  56.7 us
    pallas_call x1, Pallas kernels, on_device(): pl.pallas_call(store, out_shape=shapes, in_specs=[vmem] * 4, out_specs=(h...  2.23 us

profile of v5, /device:TPU:1, one launch (start us, length us, event | category | flops | bytes accessed | tf_op | source)
XLA Modules:
  0.0 59.5 jit_solution(5038083583827894860)
XLA Ops:
  0.6 56.7 %section.1 = (bf16[4,8,64,256]{3,2,1,0:T(8,128)(2,1)S(1)}, bf16[4,4,32,256]{3,2,1,0:T(8,128)(2,1)S(1)}, f32[288,8,256]{2,1,0:T(8,128)S(1)}, f32[96,8,256]{2,1,0:T(8,128)S(1)}) custom-call(bf16[4,4,32,256]{3,2,1,0:T(8,128)(2,1)} %bitcast.9, bf16[9,256,256]{2,1,0:T(8,128)(2,1)} %bitcast.7, bf16[3,256,256]{2,1,0:T(8,128)(2,1)} %t_hbm.1, ...), custom_call_target="tpu_custom_call" | custom-call | tf_op jit(solution)/shard_map/section/pallas_call | solution.py:526
  57.3 2.2 %store.1 = (bf16[4,8,64,256]{3,2,1,0:T(8,128)(2,1)}, bf16[4,4,32,256]{3,2,1,0:T(8,128)(2,1)}, f32[288,8,256]{2,1,0:T(8,128)}, f32[96,8,256]{2,1,0:T(8,128)}) custom-call(bf16[4,8,64,256]{3,2,1,0:T(8,128)(2,1)S(1)} %get-tuple-element.12.so_v, bf16[4,4,32,256]{3,2,1,0:T(8,128)(2,1)S(1)} %get-tuple-element.13.ig_v, f32[288,8,256]{2,1,0:T(8,128)S(1)} %get-tuple-element.14.s_v, ...), custom_call_target="tpu_custom_call" | custom-call | tf_op jit(solution)/shard_map/store/pallas_call | solution.py:537
